TPU v7x, 512 devices: a whole 4x8x8 slice. The times are simulated.
512 devices in a mesh: gossip: 16 (over z, y_lo), shard: 32 (over x, y_hi, core).
Axes of the slice: x: 4, y: 8 (y_hi: 4, y_lo: 2; y = y_hi * 2 + y_lo), z: 8, core: 2. Of those that a mesh axis runs over, the one named last changes fastest.
Arguments:
- inputs: bfloat16 [16, 13824, 2020], P('gossip', 'shard'), may hold values from -6 to 6
- upstream: bfloat16 [16, 13824, 1010], P('gossip', 'shard'), may hold values from -6 to 6
- params: float32 [16, 2048, 1010], P('gossip', 'shard'), may hold values from -0.125 to 0.125
- ps_weight: float32 [16], P('gossip'), may hold values from 0.5 to 2
- step: int32 [1], replicated, may hold values from 0 to 999
- cycle_order: int32 [16], replicated, may hold values from 0 to 15, each once
Outputs:
- grad_in: bfloat16 [16, 13824, 2020], P('gossip', 'shard')
- new_params: float32 [16, 2048, 1010], P('gossip', 'shard')
- new_weight: float32 [16], P('gossip')
Inputs may be any that keep to these rules, and one draw needn't show every extreme that they name: cycle_order names every group once.
All inputs are finite; a program needn't handle non-finite values.
Results may differ from a plain program's by a relative error of at most 0.0061.
Values may be sent and summed in bfloat16 or wider, within the bound.
No kernel may reach another device: no remote copies, remote signals or barrier semaphores. Data moves between devices by JAX's collectives and lax.ppermute only.
A program may use at most 64 MiB of HBM per device.

v0:
```python
import functools

import jax
import jax.numpy as jnp
from jax import lax
from jax.experimental import pallas as pl
from jax.experimental.pallas import tpu as pltpu
from jax.sharding import PartitionSpec as P


LEARN_RATE = 0.5
NX, NY = 4, 4
ROWS = 64
LANES = 1024
HALF = 512


def mask_of(core, j):
    return (0, 1 + 2 * core, 3 - 2 * core, 2)[j]


def place(sid):
    return sid // 8, (sid // 2) % 4, sid % 2


def pairs(axis, stage):
    out = []
    for s in range(2 * NX * NY):
        x, y, c = s // 8, (s // 2) % 4, s % 2
        if axis == "core":
            c ^= 1
        elif axis == "x":
            x ^= mask_of(c, stage)
        else:
            y ^= mask_of(c, stage)
        out.append((s, (x * NY + y) * 2 + c))
    return out


def send(v, axis, stage=0):
    return lax.ppermute(v, "shard", pairs(axis, stage))


def vmem():
    return pl.BlockSpec(memory_space=pltpu.VMEM)


def smem():
    return pl.BlockSpec(memory_space=pltpu.SMEM)


def params(mib):
    return pltpu.CompilerParams(vmem_limit_bytes=mib << 20)


def split_kernel(sid_ref, x_ref, own_ref, other_ref, wide):
    cx, _, core = place(sid_ref[0])
    rows, width = x_ref.shape
    main = width // 128 * 128
    wide[:, main:] = jnp.zeros((rows, wide.shape[1] - main), wide.dtype)
    wide[:, :main] = x_ref[:, :main]
    wide[:, main:width] = x_ref[:, main:]
    for c, out_ref in ((core, own_ref), (1 - core, other_ref)):
        for jx in range(NX):
            col = pl.multiple_of((cx ^ mask_of(c, jx)) * 512, 512)
            for q in range(2):
                t = wide[:, pl.ds(pl.multiple_of(col + 256 * q, 256), 256)].astype(jnp.float32)
                t0, t1 = t[:, :128], t[:, 128:]
                low = lax.broadcasted_iota(jnp.int32, t0.shape, 1) < 64
                even = jnp.where(low, t0, pltpu.roll(t1, 64, 1))
                odd = jnp.where(low, pltpu.roll(t0, 64, 1), t1)
                at = slice(256 * jx + 128 * q, 256 * jx + 128 * q + 128)
                out_ref[:, at] = jnp.where(c == 0, even, odd).astype(jnp.bfloat16)


def split_by_core(sid, x):
    rows = x.shape[0]
    half = jax.ShapeDtypeStruct((rows, NX * NY * ROWS), jnp.bfloat16)
    return pl.pallas_call(
        split_kernel,
        in_specs=[smem(), vmem()],
        out_specs=[vmem(), vmem()],
        out_shape=[half, half],
        scratch_shapes=[pltpu.VMEM((rows, 2 * NX * NY * ROWS), jnp.bfloat16)],
        compiler_params=params(16),
        cost_estimate=pl.CostEstimate(flops=rows * 2048 * 4, bytes_accessed=rows * 8192, transcendentals=0),
    )(sid, x)


def product_kernel(terms, first, *refs):
    xs, ws, rest = refs[:2 * terms], refs[2 * terms:3 * terms], refs[3 * terms:]
    z_ref, out_ref = (None, rest[0]) if len(rest) == 1 else rest
    rows = xs[0].shape[0]
    for block in range(2):
        at = slice(rows * block, rows * block + rows)
        for n in range(2):
            out = slice(HALF * n, HALF * n + HALF)
            z = None if z_ref is None else z_ref[at, out]
            for i in range(terms):
                x = xs[2 * i + block][:, first:first + 512]
                term = jnp.dot(x, ws[i][:, out], preferred_element_type=jnp.float32)
                z = term if z is None else z + term
            out_ref[at, out] = z


def product(first, xs, ws, z=None):
    rows = xs[0].shape[0]
    terms = len(ws)
    ops = (*xs, *ws) if z is None else (*xs, *ws, z)
    return pl.pallas_call(
        functools.partial(product_kernel, terms, first),
        in_specs=[vmem()] * len(ops),
        out_specs=vmem(),
        out_shape=jax.ShapeDtypeStruct((2 * rows, LANES), jnp.float32),
        compiler_params=params(20),
        cost_estimate=pl.CostEstimate(
            flops=4 * terms * rows * 512 * LANES, bytes_accessed=4 << 20, transcendentals=0
        ),
    )(*ops)


def forward_kernel(x_ref, xp_ref, w_ref, z_ref, up_ref, upp_ref, d_ref):
    rows, cols = up_ref.shape
    for block, (x, u_ref) in enumerate(((x_ref, up_ref), (xp_ref, upp_ref))):
        at = slice(rows * block, rows * block + rows)
        for n in range(2):
            out = slice(HALF * n, HALF * n + HALF)
            z = z_ref[at, out] + jnp.dot(x[:, 512:], w_ref[:, out], preferred_element_type=jnp.float32)
            width = min(HALF, cols - HALF * n)
            z = z[:, :width]
            s = 1.0 / (1.0 + jnp.exp(-z))
            up = u_ref[:, HALF * n:HALF * n + width].astype(jnp.float32)
            d = up * s * (1.0 + z * (1.0 - s))
            if width < HALF:
                d_ref[at, LANES - 128:] = jnp.zeros((rows, 128), jnp.bfloat16)
            d_ref[at, HALF * n:HALF * n + width] = d.astype(jnp.bfloat16)


def forward(x, x_other, w, z, up, up_other):
    rows, cols = up.shape
    return pl.pallas_call(
        forward_kernel,
        in_specs=[vmem()] * 6,
        out_specs=vmem(),
        out_shape=jax.ShapeDtypeStruct((2 * rows, LANES), jnp.bfloat16),
        compiler_params=params(24),
        cost_estimate=pl.CostEstimate(
            flops=4 * rows * 512 * cols, bytes_accessed=4 << 20, transcendentals=2 * rows * cols
        ),
        name="forward",
    )(x, x_other, w, z, up, up_other)


def back_kernel(width, sid_ref, d_ref, a0, a1, b0, b1, out_ref, wv):
    cx, _, core = place(sid_ref[0])
    rows = out_ref.shape[0]
    for k, src in enumerate((a0, a1, b0, b1)):
        c = core if k < 2 else 1 - core
        for jx in range(2):
            for jy in range(4):
                bx = cx ^ mask_of(c, jx + 2 * (k % 2))
                row = pl.multiple_of(((bx * NY + jy) * 2 + c) * ROWS, ROWS)
                at = (jx * 4 + jy) * ROWS
                wv[pl.ds(row, ROWS), :] = src[at:at + ROWS, :]
    dims = (((1,), (1,)), ((), ()))
    for n in range(4):
        g = lax.dot_general(
            d_ref[:rows], wv[512 * n:512 * n + 512], dims, preferred_element_type=jnp.float32
        )
        take = min(512, width - 512 * n)
        out_ref[:, 512 * n:512 * n + take] = g[:, :take].astype(jnp.bfloat16)


def back(sid, rows, width, d, a0, a1, b0, b1):
    return pl.pallas_call(
        functools.partial(back_kernel, width),
        in_specs=[smem()] + [vmem()] * 5,
        out_specs=vmem(),
        out_shape=jax.ShapeDtypeStruct((rows, width), jnp.bfloat16),
        scratch_shapes=[pltpu.VMEM((2048, LANES), jnp.bfloat16)],
        compiler_params=params(20),
        cost_estimate=pl.CostEstimate(flops=2 * rows * 2048 * LANES, bytes_accessed=8 << 20, transcendentals=0),
        name="back",
    )(sid, d, a0, a1, b0, b1)


def partial_kernel(first, part, x_ref, xp_ref, d_ref, out_ref):
    dims = (((0,), (0,)), ((), ()))
    rows = x_ref.shape[0]
    columns = slice(256 * first, 256 * first + 512)
    out = slice(HALF * part, HALF * part + HALF)
    r = lax.dot_general(x_ref[:, columns], d_ref[:rows, out], dims, preferred_element_type=jnp.float32)
    r = r + lax.dot_general(xp_ref[:, columns], d_ref[rows:, out], dims, preferred_element_type=jnp.float32)
    out_ref[...] = r.astype(jnp.bfloat16)


def partial(first, part, x, x_other, d):
    rows = d.shape[0]
    return pl.pallas_call(
        functools.partial(partial_kernel, first, part),
        in_specs=[vmem()] * 3,
        out_specs=vmem(),
        out_shape=jax.ShapeDtypeStruct((512, HALF), jnp.bfloat16),
        compiler_params=params(16),
        cost_estimate=pl.CostEstimate(flops=2 * rows * 512 * HALF, bytes_accessed=2 << 20, transcendentals=0),
    )(x, x_other, d)


def pack_kernel(scale, sid_ref, w_ref, p_ref, ka_ref, ga_ref, kb_ref, gb_ref, own_ref, pack_ref):
    _, cy, _ = place(sid_ref[0])
    _, cols = p_ref.shape
    tail = cols - 7 * 128
    w = jnp.full((32, 128), w_ref[0], jnp.float32)
    hi = w.astype(jnp.bfloat16).astype(jnp.float32)
    lane = lax.broadcasted_iota(jnp.int32, (32, 128), 1)
    spare = jnp.where(lane == 126, hi, jnp.where(lane == 127, w - hi, 0.0)).astype(jnp.bfloat16)
    for y in range(NY):
        at = slice(ROWS * y, ROWS * y + ROWS)
        v = jnp.concatenate(
            [
                scale * (keep_ref[at].astype(jnp.float32) + got_ref[at].astype(jnp.float32))
                for keep_ref, got_ref in ((ka_ref, ga_ref), (kb_ref, gb_ref))
            ],
            axis=1,
        )
        for h in range(2):
            for j in range(8):
                pack_ref[y * 16 + 8 * h + j] = v[32 * h:32 * h + 32, 128 * j:128 * j + 128].astype(jnp.bfloat16)
    at = pl.ds(pl.multiple_of(cy * ROWS, ROWS), ROWS)
    v = jnp.concatenate(
        [
            scale * (keep_ref[at].astype(jnp.float32) + got_ref[at].astype(jnp.float32))
            for keep_ref, got_ref in ((ka_ref, ga_ref), (kb_ref, gb_ref))
        ],
        axis=1,
    )
    own = p_ref[...] + v[:, :cols]
    own_ref[...] = own
    for h in range(2):
        for j in range(8):
            to = cy * 16 + 8 * h + j
            if j == 7:
                pack_ref[to] = spare
                pack_ref[to, :, :tail] = own[32 * h:32 * h + 32, 896:].astype(jnp.bfloat16)
            else:
                pack_ref[to] = own[32 * h:32 * h + 32, 128 * j:128 * j + 128].astype(jnp.bfloat16)


def pack(scale, sid, weight, own, *sums):
    return pl.pallas_call(
        functools.partial(pack_kernel, scale),
        in_specs=[smem(), smem()] + [vmem()] * 5,
        out_specs=[vmem(), vmem()],
        out_shape=[
            jax.ShapeDtypeStruct(own.shape, jnp.float32),
            jax.ShapeDtypeStruct((64, 32, 128), jnp.bfloat16),
        ],
        compiler_params=params(8),
        cost_estimate=pl.CostEstimate(flops=1 << 20, bytes_accessed=2 << 20, transcendentals=0),
        name="pack",
    )(sid, weight, own, *sums)


def mix_kernel(sid_ref, gid_ref, step_ref, order_ref, in_ref, out_ref, total):
    _, cy, _ = place(sid_ref[0])
    for g in range(16):
        t = in_ref[g].astype(jnp.float32)
        for y in range(1, NY):
            t = t + in_ref[16 * y + g].astype(jnp.float32)
        total[g] = t
    lane = lax.broadcasted_iota(jnp.int32, (32, 128), 1)
    spare = (lane >= 126) & (gid_ref[0] % 8 == 7)
    distance = 1 << lax.rem(step_ref[0], 4)
    for p in range(16):
        m = order_ref[p]
        source = total[order_ref[(p - distance + 16) % 16]]
        rest = total[m] - in_ref[16 * cy + m].astype(jnp.float32)
        out_ref[m] = jnp.where(spare, source, 0.5 * (source + rest)).astype(jnp.bfloat16)


def mix(sid, gid, step, order, got):
    return pl.pallas_call(
        mix_kernel,
        in_specs=[smem()] * 4 + [vmem()],
        out_specs=vmem(),
        out_shape=jax.ShapeDtypeStruct((16, 32, 128), jnp.bfloat16),
        scratch_shapes=[pltpu.VMEM((16, 32, 128), jnp.float32)],
        compiler_params=params(8),
        cost_estimate=pl.CostEstimate(flops=1 << 20, bytes_accessed=1 << 20, transcendentals=0),
        name="mix",
    )(sid, gid, step, order, got)


def finish_kernel(w_ref, own_ref, got_ref, new_ref, new_w_ref):
    _, cols = own_ref.shape
    for h in range(2):
        for j in range(8):
            width = min(128, cols - 128 * j)
            at = (slice(32 * h, 32 * h + 32), slice(128 * j, 128 * j + width))
            new_ref[at] = 0.5 * own_ref[at] + got_ref[8 * h + j].astype(jnp.float32)[:, :width]
    last = got_ref[7].astype(jnp.float32)
    lane = lax.broadcasted_iota(jnp.int32, last.shape, 1)
    row = lax.broadcasted_iota(jnp.int32, last.shape, 0)
    source_w = jnp.sum(jnp.where((lane >= 126) & (row == 0), last, 0.0))
    new_w_ref[0] = 0.5 * w_ref[0] + 0.5 * source_w


def finish(weight, own, got):
    return pl.pallas_call(
        finish_kernel,
        in_specs=[smem(), vmem(), vmem()],
        out_specs=[vmem(), smem()],
        out_shape=[
            jax.ShapeDtypeStruct(own.shape, jnp.float32),
            jax.ShapeDtypeStruct((1,), jnp.float32),
        ],
        compiler_params=params(8),
        name="finish",
    )(weight, own, got)


def add(a, b):
    return (a.astype(jnp.float32) + b.astype(jnp.float32)).astype(jnp.bfloat16)


def halves(a):
    n = a.shape[0] // 2
    return a[:n], a[n:]


def body(inputs, upstream, params, ps_weight, step, cycle_order):
    x_rows = inputs[0]
    up_rows = upstream[0]
    own_shard = params[0]
    n_shard = lax.axis_size("shard")
    n_groups = lax.axis_size("gossip")
    in_width = x_rows.shape[1]
    sid = lax.axis_index("shard").astype(jnp.int32).reshape(1)

    debiased = (own_shard / ps_weight[0]).astype(jnp.bfloat16)
    debiased = jnp.pad(debiased, ((0, 0), (0, LANES - debiased.shape[1])))
    columns = [[(x * NY + y) * 2 + c for y in range(NY)] for x in range(NX) for c in range(2)]
    held = lax.all_gather(debiased, "shard", axis=0, axis_index_groups=columns, tiled=True)
    held, x_rows, up_rows = lax.optimization_barrier((held, x_rows, up_rows))
    got = send(held, "x", 1)
    x_other = send(x_rows, "core")
    xa, xb = split_by_core(sid, x_rows)
    got, xa, xb = lax.optimization_barrier((got, xa, xb))
    held = jnp.concatenate([held, got])
    up_other = send(up_rows, "core")
    far = send(held, "x", 2)
    other_held = send(held, "core")
    ya, yb = split_by_core(sid, x_other)
    z = product(0, (xa, ya, xb, yb), (held, other_held))
    far, z, up_other = lax.optimization_barrier((far, z, up_other))
    other_far = send(far, "core")
    weights = (held, far, other_held, other_far)
    z = product(512, (xa, ya), (far,), z)
    d_pre = forward(xb, yb, other_far, z, up_rows, up_other)
    got = [send(partial(2, i, xa, ya, d_pre), "x", 2) for i in range(2)]
    keep = [partial(0, i, xa, ya, d_pre) for i in range(2)]
    sums = []
    for i in range(2):
        (k0, k1), (g0, g1) = halves(keep[i]), halves(got[i])
        sums.extend([add(k0, g0), send(add(k1, g1), "x", 1)])
    grad_in = back(sid, x_rows.shape[0], in_width, d_pre, *weights)
    sums[3], grad_in = lax.optimization_barrier((sums[3], grad_in))

    tokens = x_rows.shape[0] * n_shard
    gid = lax.axis_index("gossip").astype(jnp.int32).reshape(1)
    own, pieces = pack(-LEARN_RATE / tokens, sid, ps_weight, own_shard, *sums)
    planes = [
        [g * n_shard + (x * NY + y) * 2 + c for y in range(NY) for g in range(n_groups)]
        for x in range(NX) for c in range(2)
    ]
    received = lax.all_to_all(
        pieces, ("gossip", "shard"), split_axis=0, concat_axis=0, axis_index_groups=planes, tiled=True
    )
    outgoing = mix(sid, gid, step, cycle_order, received)
    arrived = lax.all_to_all(outgoing, "gossip", split_axis=0, concat_axis=0, tiled=True)
    new_params, new_weight = finish(ps_weight, own, arrived)
    return (grad_in[None], new_params[None], new_weight)


def solution(mesh):
    placed = (
        P("gossip", "shard", None),
        P("gossip", "shard", None),
        P("gossip", "shard", None),
        P("gossip"),
        P(),
        P(),
    )

    return jax.shard_map(
        body,
        mesh=mesh,
        in_specs=placed,
        out_specs=(P("gossip", "shard", None), P("gossip", "shard", None), P("gossip")),
        check_vma=False,
    )
```

profile of v0, /device:TPU:6, one launch (start us, length us, event | category | flops | bytes accessed | tf_op | source)
XLA Modules:
  0.0 136.2 jit_solution(16661016441908829844)
XLA Ops:
  1.3 1.0 divide_convert_fusion
  2.3 20.0 %all_gather.3 = bf16[256,1024]{1,0:T(8,128)(2,1)S(1)} all-gather(bf16[64,1024]{1,0:T(8,128)(2,1)S(1)} %pad.4), channel_id=1, replica_groups={{0,2,4,6},{1,3,5,7},{8,10,12,14},{9,11,13,15},{16,18,20,22},{17,19,21,2..., dimensions={0}, use_global_device_ids=true | all-gather | bytes 655360 | tf_op jit(solution)/shard_map/all_gather | solution.py:343
  22.3 1.9 %collective-permute-start.1 = (bf16[432,2020]{1,0:T(8,128)(2,1)}, bf16[432,2020]{1,0:T(8,128)(2,1)S(1)}, u32[]{:S(2)}, u32[]{:S(2)}) collective-permute-start(bf16[432,2020]{1,0:T(8,128)(2,1)} %bitcast.10), channel_id=1, source_target_pairs={{0,1},{1,0},{2,3},{3,2},{4,5},{5,4},{6,7},{7,6},{8,9},{9,8},{10,11... | collective-permute-start | bytes 5235848 | tf_op jit(solution)/shard_map/ppermute | solution.py:41
  24.2 2.7 %collective-permute-start = (bf16[256,1024]{1,0:T(8,128)(2,1)S(1)}, bf16[256,1024]{1,0:T(8,128)(2,1)S(1)}, u32[]{:S(2)}, u32[]{:S(2)}) collective-permute-start(bf16[256,1024]{1,0:T(8,128)(2,1)S(1)} %all_gather.3), channel_id=1, source_target_pairs={{0,8},{1,25},{2,10},{3,27},{4,12},{5,29},{6,14},{7,31},{8,0},{9,17... | collective-permute-start | bytes 1572872 | tf_op jit(solution)/shard_map/ppermute | solution.py:41
  26.9 1.5 %copy-done = bf16[1,432,2020]{2,1,0:T(8,128)(2,1)S(1)} copy-done((bf16[1,432,2020]{2,1,0:T(8,128)(2,1)S(1)}, bf16[1,432,2020]{2,1,0:T(8,128)(2,1)}, u32[]{:S(2)}) %copy-start) | copy-done | bytes 1745304
  28.4 1.8 %shard_map.85 = (bf16[432,1024]{1,0:T(8,128)(2,1)S(1)}, bf16[432,1024]{1,0:T(8,128)(2,1)S(1)}) custom-call(s32[1]{0:T(128)} %bitcast.4.sid_ref, bf16[432,2020]{1,0:T(8,128)(2,1)S(1)} %bitcast.11), custom_call_target="tpu_custom_call" | custom-call | flops 3538944 | bytes 3538944 | tf_op jit(solution)/shard_map/pallas_call | solution.py:79
  30.2 5.0 %collective-permute-done = bf16[256,1024]{1,0:T(8,128)(2,1)S(1)} collective-permute-done((bf16[256,1024]{1,0:T(8,128)(2,1)S(1)}, bf16[256,1024]{1,0:T(8,128)(2,1)S(1)}, u32[]{:S(2)}, u32[]{:S(2)}) %collective-permute-start) | collective-permute-done | bytes 524320 | tf_op jit(solution)/shard_map/ppermute | solution.py:41
  35.3 2.5 %collective-permute-start.3 = (bf16[512,1024]{1,0:T(8,128)(2,1)S(1)}, bf16[512,1024]{1,0:T(8,128)(2,1)S(1)}, u32[]{:S(2)}, u32[]{:S(2)}) collective-permute-start(bf16[512,1024]{1,0:T(8,128)(2,1)S(1)} %constant_dynamic-update-slice_fusion.refs_4_.a0), channel_id=1, source_target_pairs={{0,1},{1,0},{2,3},{3,2},{4,5},{5,4},{6,7},{7,6},{8,9},{9,8},{10,11... | collective-permute-start | bytes 3145736 | tf_op jit(solution)/shard_map/ppermute | solution.py:41
  37.8 3.2 %collective-permute-start.2 = (bf16[512,1024]{1,0:T(8,128)(2,1)S(1)}, bf16[512,1024]{1,0:T(8,128)(2,1)S(1)}, u32[]{:S(2)}, u32[]{:S(2)}) collective-permute-start(bf16[512,1024]{1,0:T(8,128)(2,1)S(1)} %constant_dynamic-update-slice_fusion.refs_4_.a0), channel_id=1, source_target_pairs={{0,24},{1,9},{2,26},{3,11},{4,28},{5,13},{6,30},{7,15},{8,16},{9,1... | collective-permute-start | bytes 3145736 | tf_op jit(solution)/shard_map/ppermute | solution.py:41
  41.0 1.9 %collective-permute-start.4 = (bf16[432,1010]{1,0:T(8,128)(2,1)S(1)}, bf16[432,1010]{1,0:T(8,128)(2,1)S(1)}, u32[]{:S(2)}, u32[]{:S(2)}) collective-permute-start(bf16[432,1010]{1,0:T(8,128)(2,1)S(1)} %bitcast.13), channel_id=1, source_target_pairs={{0,1},{1,0},{2,3},{3,2},{4,5},{5,4},{6,7},{7,6},{8,9},{9,8},{10,11... | collective-permute-start | bytes 2617928 | tf_op jit(solution)/shard_map/ppermute | solution.py:41
  43.0 1.8 %shard_map.86 = (bf16[432,1024]{1,0:T(8,128)(2,1)S(1)}, bf16[432,1024]{1,0:T(8,128)(2,1)S(1)}) custom-call(s32[1]{0:T(128)} %bitcast.4.sid_ref, bf16[432,2020]{1,0:T(8,128)(2,1)S(1)} %collective-permute-done.1.x_ref), custom_call_target="tpu_custom_call" | custom-call | flops 3538944 | bytes 3538944 | tf_op jit(solution)/shard_map/pallas_call | solution.py:79
  44.8 2.0 %shard_map.87.refs_3_ = f32[864,1024]{1,0:T(8,128)S(1)} custom-call(bf16[432,1024]{1,0:T(8,128)(2,1)S(1)} %get-tuple-element.26.refs_0_.x_ref, bf16[432,1024]{1,0:T(8,128)(2,1)S(1)} %get-tuple-element.27.refs_1_.xp_ref, bf16[432,1024]{1,0:T(8,128)(2,1)S(1)} %get-tuple-element.28.refs_2_.x_ref, bf16[432,1024]{1,0:T(8,128)(2,1)S(1)} %get-tuple-element.29.refs_3_.xp_ref, ...), custom_call_target="tpu_custom_call" | custom-call | flops 1811939328 | bytes 4194304 | tf_op jit(solution)/shard_map/pallas_call | solution.py:110
  46.8 8.9 %collective-permute-done.2.refs_2_.a1 = bf16[512,1024]{1,0:T(8,128)(2,1)S(1)} collective-permute-done((bf16[512,1024]{1,0:T(8,128)(2,1)S(1)}, bf16[512,1024]{1,0:T(8,128)(2,1)S(1)}, u32[]{:S(2)}, u32[]{:S(2)}) %collective-permute-start.2) | collective-permute-done | bytes 1048608 | tf_op jit(solution)/shard_map/ppermute | solution.py:41
  55.7 1.9 %collective-permute-start.5 = (bf16[512,1024]{1,0:T(8,128)(2,1)S(1)}, bf16[512,1024]{1,0:T(8,128)(2,1)S(1)}, u32[]{:S(2)}, u32[]{:S(2)}) collective-permute-start(bf16[512,1024]{1,0:T(8,128)(2,1)S(1)} %collective-permute-done.2.refs_2_.a1), channel_id=1, source_target_pairs={{0,1},{1,0},{2,3},{3,2},{4,5},{5,4},{6,7},{7,6},{8,9},{9,8},{10,11... | collective-permute-start | bytes 3145736 | tf_op jit(solution)/shard_map/ppermute | solution.py:41
  57.6 1.1 shard_map.88.z_ref
  58.7 1.5 %collective-permute-done.5.w_ref.b1 = bf16[512,1024]{1,0:T(8,128)(2,1)S(1)} collective-permute-done((bf16[512,1024]{1,0:T(8,128)(2,1)S(1)}, bf16[512,1024]{1,0:T(8,128)(2,1)S(1)}, u32[]{:S(2)}, u32[]{:S(2)}) %collective-permute-start.5) | collective-permute-done | bytes 1048608 | tf_op jit(solution)/shard_map/ppermute | solution.py:41
  60.2 2.2 %forward.1.d_ref = bf16[864,1024]{1,0:T(8,128)(2,1)S(1)} custom-call(bf16[432,1024]{1,0:T(8,128)(2,1)S(1)} %get-tuple-element.28.refs_2_.x_ref, bf16[432,1024]{1,0:T(8,128)(2,1)S(1)} %get-tuple-element.29.refs_3_.xp_ref, bf16[512,1024]{1,0:T(8,128)(2,1)S(1)} %collective-permute-done.5.w_ref.b1, f32[864,1024]{1,0:T(8,128)S(1)} %shard_map.88.z_ref, ...), custom_call_target="tpu_custom_call" | custom-call | flops 893583360 | bytes 4194304 | tf_op jit(solution)/shard_map/forward/pallas_call | solution.py:141
  62.5 0.7 shard_map.90
  63.2 3.2 %collective-permute-start.6 = (bf16[512,512]{1,0:T(8,128)(2,1)S(1)}, bf16[512,512]{1,0:T(8,128)(2,1)S(1)}, u32[]{:S(2)}, u32[]{:S(2)}) collective-permute-start(bf16[512,512]{1,0:T(8,128)(2,1)S(1)} %shard_map.90), channel_id=1, source_target_pairs={{0,24},{1,9},{2,26},{3,11},{4,28},{5,13},{6,30},{7,15},{8,16},{9,1... | collective-permute-start | bytes 1572872 | tf_op jit(solution)/shard_map/ppermute | solution.py:41
  66.5 0.7 shard_map.92
  67.2 3.8 %collective-permute-start.8 = (bf16[512,512]{1,0:T(8,128)(2,1)S(1)}, bf16[512,512]{1,0:T(8,128)(2,1)S(1)}, u32[]{:S(2)}, u32[]{:S(2)}) collective-permute-start(bf16[512,512]{1,0:T(8,128)(2,1)S(1)} %shard_map.92), channel_id=1, source_target_pairs={{0,24},{1,9},{2,26},{3,11},{4,28},{5,13},{6,30},{7,15},{8,16},{9,1... | collective-permute-start | bytes 1572872 | tf_op jit(solution)/shard_map/ppermute | solution.py:41
  71.0 0.7 shard_map.91
  72.5 3.0 %collective-permute-done.6 = bf16[512,512]{1,0:T(8,128)(2,1)S(1)} collective-permute-done((bf16[512,512]{1,0:T(8,128)(2,1)S(1)}, bf16[512,512]{1,0:T(8,128)(2,1)S(1)}, u32[]{:S(2)}, u32[]{:S(2)}) %collective-permute-start.6) | collective-permute-done | bytes 524320 | tf_op jit(solution)/shard_map/ppermute | solution.py:41
  75.6 1.9 %collective-permute-start.7 = (bf16[256,512]{1,0:T(8,128)(2,1)S(1)}, bf16[256,512]{1,0:T(8,128)(2,1)S(1)}, u32[]{:S(2)}, u32[]{:S(2)}) collective-permute-start(bf16[256,512]{1,0:T(8,128)(2,1)S(1)} %get-tuple-element.42), channel_id=1, source_target_pairs={{0,8},{1,25},{2,10},{3,27},{4,12},{5,29},{6,14},{7,31},{8,0},{9,17... | collective-permute-start | bytes 786440 | tf_op jit(solution)/shard_map/ppermute | solution.py:41
  77.6 5.3 %collective-permute-done.8 = bf16[512,512]{1,0:T(8,128)(2,1)S(1)} collective-permute-done((bf16[512,512]{1,0:T(8,128)(2,1)S(1)}, bf16[512,512]{1,0:T(8,128)(2,1)S(1)}, u32[]{:S(2)}, u32[]{:S(2)}) %collective-permute-start.8) | collective-permute-done | bytes 524320 | tf_op jit(solution)/shard_map/ppermute | solution.py:41
  83.0 2.2 %collective-permute-start.9 = (bf16[256,512]{1,0:T(8,128)(2,1)S(1)}, bf16[256,512]{1,0:T(8,128)(2,1)S(1)}, u32[]{:S(2)}, u32[]{:S(2)}) collective-permute-start(bf16[256,512]{1,0:T(8,128)(2,1)S(1)} %get-tuple-element.43), channel_id=1, source_target_pairs={{0,8},{1,25},{2,10},{3,27},{4,12},{5,29},{6,14},{7,31},{8,0},{9,17... | collective-permute-start | bytes 786440 | tf_op jit(solution)/shard_map/ppermute | solution.py:41
  85.2 3.5 %back.1 = bf16[432,2020]{1,0:T(8,128)(2,1)} custom-call(s32[1]{0:T(128)} %bitcast.4.sid_ref, bf16[864,1024]{1,0:T(8,128)(2,1)S(1)} %forward.1.d_ref, bf16[512,1024]{1,0:T(8,128)(2,1)S(1)} %constant_dynamic-update-slice_fusion.refs_4_.a0, bf16[512,1024]{1,0:T(8,128)(2,1)S(1)} %collective-permute-done.2.refs_2_.a1, ...), custom_call_target="tpu_custom_call" | custom-call | flops 1811939328 | bytes 8388608 | tf_op jit(solution)/shard_map/back/pallas_call | solution.py:175
  88.7 2.6 %collective-permute-done.9.ga_ref = bf16[256,512]{1,0:T(8,128)(2,1)S(1)} collective-permute-done((bf16[256,512]{1,0:T(8,128)(2,1)S(1)}, bf16[256,512]{1,0:T(8,128)(2,1)S(1)}, u32[]{:S(2)}, u32[]{:S(2)}) %collective-permute-start.9) | collective-permute-done | bytes 262176 | tf_op jit(solution)/shard_map/ppermute | solution.py:41
  91.4 1.0 pack.1
  92.4 13.2 %all-to-all-start = ((bf16[64,32,128]{2,1,0:T(8,128)(2,1)}), bf16[64,32,128]{2,1,0:T(8,128)(2,1)S(1)}, u32[]{:S(2)}, u32[]{:S(2)}) async-start(bf16[64,32,128]{2,1,0:T(8,128)(2,1)} %get-tuple-element.38), calls=%async_computation | async-start | bytes 1048576 | tf_op jit(solution)/shard_map/all_to_all | solution.py:376
  106.2 14.2 %all-to-all-done.in_ref = bf16[64,32,128]{2,1,0:T(8,128)(2,1)S(1)} async-done(((bf16[64,32,128]{2,1,0:T(8,128)(2,1)}), bf16[64,32,128]{2,1,0:T(8,128)(2,1)S(1)}, u32[]{:S(2)}, u32[]{:S(2)}) %all-to-all-start) | async-done | bytes 524320 | tf_op jit(solution)/shard_map/all_to_all | solution.py:376
  121.1 14.2 %all_to_all.10.got_ref = bf16[16,32,128]{2,1,0:T(8,128)(2,1)S(1)} all-to-all(bf16[16,32,128]{2,1,0:T(8,128)(2,1)S(1)} %mix.1), channel_id=1, replica_groups=mesh['gossip'=16,'shard'=32] {'gossip'}, dimensions={0} | all-to-all | bytes 262144 | tf_op jit(solution)/shard_map/all_to_all | solution.py:380
  (19 shorter events, 2.5 us)
Async XLA Ops:
  22.3 20.7 %collective-permute-start.1 = (bf16[432,2020]{1,0:T(8,128)(2,1)}, bf16[432,2020]{1,0:T(8,128)(2,1)S(1)}, u32[]{:S(2)}, u32[]{:S(2)}) collective-permute-start(bf16[432,2020]{1,0:T(8,128)(2,1)} %bitcast.10), channel_id=1, source_target_pairs={{0,1},{1,0},{2,3},{3,2},{4,5},{5,4},{6,7},{7,6},{8,9},{9,8},{10,11... | collective-permute-start | bytes 5235848 | tf_op jit(solution)/shard_map/ppermute | solution.py:41
  24.2 11.1 %collective-permute-start = (bf16[256,1024]{1,0:T(8,128)(2,1)S(1)}, bf16[256,1024]{1,0:T(8,128)(2,1)S(1)}, u32[]{:S(2)}, u32[]{:S(2)}) collective-permute-start(bf16[256,1024]{1,0:T(8,128)(2,1)S(1)} %all_gather.3), channel_id=1, source_target_pairs={{0,8},{1,25},{2,10},{3,27},{4,12},{5,29},{6,14},{7,31},{8,0},{9,17... | collective-permute-start | bytes 1572872 | tf_op jit(solution)/shard_map/ppermute | solution.py:41
  26.9 1.5 %copy-start = (bf16[1,432,2020]{2,1,0:T(8,128)(2,1)S(1)}, bf16[1,432,2020]{2,1,0:T(8,128)(2,1)}, u32[]{:S(2)}) copy-start(bf16[1,432,2020]{2,1,0:T(8,128)(2,1)} %param.6) | copy-start | bytes 5235844
  28.4 12.6 %copy-start.2 = (bf16[1,432,1010]{2,1,0:T(8,128)(2,1)S(1)}, bf16[1,432,1010]{2,1,0:T(8,128)(2,1)}, u32[]{:S(2)}) copy-start(bf16[1,432,1010]{2,1,0:T(8,128)(2,1)} %param.7) | copy-start | bytes 2617924
  35.3 9.5 %collective-permute-start.3 = (bf16[512,1024]{1,0:T(8,128)(2,1)S(1)}, bf16[512,1024]{1,0:T(8,128)(2,1)S(1)}, u32[]{:S(2)}, u32[]{:S(2)}) collective-permute-start(bf16[512,1024]{1,0:T(8,128)(2,1)S(1)} %constant_dynamic-update-slice_fusion.refs_4_.a0), channel_id=1, source_target_pairs={{0,1},{1,0},{2,3},{3,2},{4,5},{5,4},{6,7},{7,6},{8,9},{9,8},{10,11... | collective-permute-start | bytes 3145736 | tf_op jit(solution)/shard_map/ppermute | solution.py:41
  37.8 17.9 %collective-permute-start.2 = (bf16[512,1024]{1,0:T(8,128)(2,1)S(1)}, bf16[512,1024]{1,0:T(8,128)(2,1)S(1)}, u32[]{:S(2)}, u32[]{:S(2)}) collective-permute-start(bf16[512,1024]{1,0:T(8,128)(2,1)S(1)} %constant_dynamic-update-slice_fusion.refs_4_.a0), channel_id=1, source_target_pairs={{0,24},{1,9},{2,26},{3,11},{4,28},{5,13},{6,30},{7,15},{8,16},{9,1... | collective-permute-start | bytes 3145736 | tf_op jit(solution)/shard_map/ppermute | solution.py:41
  41.0 5.7 %collective-permute-start.4 = (bf16[432,1010]{1,0:T(8,128)(2,1)S(1)}, bf16[432,1010]{1,0:T(8,128)(2,1)S(1)}, u32[]{:S(2)}, u32[]{:S(2)}) collective-permute-start(bf16[432,1010]{1,0:T(8,128)(2,1)S(1)} %bitcast.13), channel_id=1, source_target_pairs={{0,1},{1,0},{2,3},{3,2},{4,5},{5,4},{6,7},{7,6},{8,9},{9,8},{10,11... | collective-permute-start | bytes 2617928 | tf_op jit(solution)/shard_map/ppermute | solution.py:41
  55.7 4.5 %collective-permute-start.5 = (bf16[512,1024]{1,0:T(8,128)(2,1)S(1)}, bf16[512,1024]{1,0:T(8,128)(2,1)S(1)}, u32[]{:S(2)}, u32[]{:S(2)}) collective-permute-start(bf16[512,1024]{1,0:T(8,128)(2,1)S(1)} %collective-permute-done.2.refs_2_.a1), channel_id=1, source_target_pairs={{0,1},{1,0},{2,3},{3,2},{4,5},{5,4},{6,7},{7,6},{8,9},{9,8},{10,11... | collective-permute-start | bytes 3145736 | tf_op jit(solution)/shard_map/ppermute | solution.py:41
  63.2 12.3 %collective-permute-start.6 = (bf16[512,512]{1,0:T(8,128)(2,1)S(1)}, bf16[512,512]{1,0:T(8,128)(2,1)S(1)}, u32[]{:S(2)}, u32[]{:S(2)}) collective-permute-start(bf16[512,512]{1,0:T(8,128)(2,1)S(1)} %shard_map.90), channel_id=1, source_target_pairs={{0,24},{1,9},{2,26},{3,11},{4,28},{5,13},{6,30},{7,15},{8,16},{9,1... | collective-permute-start | bytes 1572872 | tf_op jit(solution)/shard_map/ppermute | solution.py:41
  67.2 15.6 %collective-permute-start.8 = (bf16[512,512]{1,0:T(8,128)(2,1)S(1)}, bf16[512,512]{1,0:T(8,128)(2,1)S(1)}, u32[]{:S(2)}, u32[]{:S(2)}) collective-permute-start(bf16[512,512]{1,0:T(8,128)(2,1)S(1)} %shard_map.92), channel_id=1, source_target_pairs={{0,24},{1,9},{2,26},{3,11},{4,28},{5,13},{6,30},{7,15},{8,16},{9,1... | collective-permute-start | bytes 1572872 | tf_op jit(solution)/shard_map/ppermute | solution.py:41
  75.6 13.1 %collective-permute-start.7 = (bf16[256,512]{1,0:T(8,128)(2,1)S(1)}, bf16[256,512]{1,0:T(8,128)(2,1)S(1)}, u32[]{:S(2)}, u32[]{:S(2)}) collective-permute-start(bf16[256,512]{1,0:T(8,128)(2,1)S(1)} %get-tuple-element.42), channel_id=1, source_target_pairs={{0,8},{1,25},{2,10},{3,27},{4,12},{5,29},{6,14},{7,31},{8,0},{9,17... | collective-permute-start | bytes 786440 | tf_op jit(solution)/shard_map/ppermute | solution.py:41
  82.9 8.4 %copy-start.1 = (f32[1,64,1010]{2,1,0:T(8,128)S(1)}, f32[1,64,1010]{2,1,0:T(8,128)}, u32[]{:S(2)}) copy-start(f32[1,64,1010]{2,1,0:T(8,128)} %param.8) | copy-start | bytes 775684
  83.0 8.4 %collective-permute-start.9 = (bf16[256,512]{1,0:T(8,128)(2,1)S(1)}, bf16[256,512]{1,0:T(8,128)(2,1)S(1)}, u32[]{:S(2)}, u32[]{:S(2)}) collective-permute-start(bf16[256,512]{1,0:T(8,128)(2,1)S(1)} %get-tuple-element.43), channel_id=1, source_target_pairs={{0,8},{1,25},{2,10},{3,27},{4,12},{5,29},{6,14},{7,31},{8,0},{9,17... | collective-permute-start | bytes 786440 | tf_op jit(solution)/shard_map/ppermute | solution.py:41
  88.7 31.7 %copy-start.3 = (s32[16]{0:T(128)S(1)}, s32[16]{0:T(128)}, u32[]{:S(2)}) copy-start(s32[16]{0:T(128)} %order_ref.1) | copy-start | bytes 196
  92.4 28.0 %all-to-all-start = ((bf16[64,32,128]{2,1,0:T(8,128)(2,1)}), bf16[64,32,128]{2,1,0:T(8,128)(2,1)S(1)}, u32[]{:S(2)}, u32[]{:S(2)}) async-start(bf16[64,32,128]{2,1,0:T(8,128)(2,1)} %get-tuple-element.38), calls=%async_computation | async-start | bytes 1048576 | tf_op jit(solution)/shard_map/all_to_all | solution.py:376
where the time goes:
time: 137 us; the launch traced here: 136 us
  waiting for transfers between devices  40.5 us (30%)
  starting transfers between devices  38.6 us (28%)
  blocking collectives  34.2 us (25%)
  Pallas kernels  17.8 us (13%)
  between operations  2.34 us (2%)
  local copies, waits for them, and re-layouts  1.57 us (1%)
    ppermute x10, waiting for transfers between devices, send(): return lax.ppermute(v, 'shard', pairs(axis, stage))  26.3 us
    ppermute x10, starting transfers between devices, send(): return lax.ppermute(v, 'shard', pairs(axis, stage))  25.4 us
    all_gather x1, blocking collectives, body(): lax.all_gather(debiased, 'shard', axis=0, axis_index_groups=columns, tile...  20 us
    all_to_all x1, blocking collectives, body(): lax.all_to_all(outgoing, 'gossip', split_axis=0, concat_axis=0, tiled=True)  14.2 us
    all_to_all x1, waiting for transfers between devices, body(): lax.all_to_all(pieces, ('gossip', 'shard'), split_axis=0, concat_axis=0,...  14.2 us
    all_to_all x1, starting transfers between devices, body(): lax.all_to_all(pieces, ('gossip', 'shard'), split_axis=0, concat_axis=0,...  13.2 us
    pallas_call x2, Pallas kernels, split_by_core(): pl.pallas_call(split_kernel, in_specs=[smem(), vmem()], out_specs=[vmem()...  3.56 us
    pallas_call x1, Pallas kernels, back(): pl.pallas_call(functools.partial(back_kernel, width), in_specs=[smem()] +...  3.52 us
  transfers between devices with their start and end apart: 11, of which 7 were waited for; matrix products, arithmetic and copies ran while one was open for 0% of the time, Pallas kernels for 9%

commit v1 on v0

--- a/solution.py
+++ b/solution.py
@@ -87,117 +87,129 @@
     )(sid, x)
 
 
-def product_kernel(terms, first, *refs):
-    xs, ws, rest = refs[:2 * terms], refs[2 * terms:3 * terms], refs[3 * terms:]
-    z_ref, out_ref = (None, rest[0]) if len(rest) == 1 else rest
-    rows = xs[0].shape[0]
-    for block in range(2):
+def product_kernel(xa_ref, ya_ref, xb_ref, yb_ref, wa_ref, wb_ref, z_ref):
+    rows = xa_ref.shape[0]
+    for block, (own, other) in enumerate(((xa_ref, xb_ref), (ya_ref, yb_ref))):
         at = slice(rows * block, rows * block + rows)
         for n in range(2):
             out = slice(HALF * n, HALF * n + HALF)
-            z = None if z_ref is None else z_ref[at, out]
-            for i in range(terms):
-                x = xs[2 * i + block][:, first:first + 512]
-                term = jnp.dot(x, ws[i][:, out], preferred_element_type=jnp.float32)
-                z = term if z is None else z + term
-            out_ref[at, out] = z
-
-
-def product(first, xs, ws, z=None):
-    rows = xs[0].shape[0]
-    terms = len(ws)
-    ops = (*xs, *ws) if z is None else (*xs, *ws, z)
-    return pl.pallas_call(
-        functools.partial(product_kernel, terms, first),
-        in_specs=[vmem()] * len(ops),
+            z = jnp.dot(own[:, :512], wa_ref[:, out], preferred_element_type=jnp.float32)
+            z_ref[at, out] = z + jnp.dot(other[:, :512], wb_ref[:, out], preferred_element_type=jnp.float32)
+
+
+def product(xa, ya, xb, yb, wa, wb):
+    rows = xa.shape[0]
+    return pl.pallas_call(
+        product_kernel,
+        in_specs=[vmem()] * 6,
         out_specs=vmem(),
         out_shape=jax.ShapeDtypeStruct((2 * rows, LANES), jnp.float32),
         compiler_params=params(20),
+        cost_estimate=pl.CostEstimate(flops=8 * rows * 512 * LANES, bytes_accessed=4 << 20, transcendentals=0),
+        name="product_held",
+    )(xa, ya, xb, yb, wa, wb)
+
+
+def product_far_kernel(part, x_ref, y_ref, w_ref, z_ref, out_ref):
+    rows = x_ref.shape[0]
+    columns = slice(HALF * part, HALF * part + HALF)
+    for block, x in enumerate((x_ref, y_ref)):
+        at = slice(rows * block, rows * block + rows)
+        out_ref[at] = z_ref[at, columns] + jnp.dot(
+            x[:, 512:], w_ref[...], preferred_element_type=jnp.float32
+        )
+
+
+def product_far(part, x, y, w, z):
+    rows = x.shape[0]
+    return pl.pallas_call(
+        functools.partial(product_far_kernel, part),
+        in_specs=[vmem()] * 4,
+        out_specs=vmem(),
+        out_shape=jax.ShapeDtypeStruct((2 * rows, HALF), jnp.float32),
+        compiler_params=params(16),
+        cost_estimate=pl.CostEstimate(flops=4 * rows * 512 * HALF, bytes_accessed=2 << 20, transcendentals=0),
+    )(x, y, w, z)
+
+
+def forward_kernel(part, x_ref, y_ref, w_ref, z_ref, up_ref, upp_ref, d_ref):
+    rows, cols = up_ref.shape
+    first = HALF * part
+    width = min(HALF, cols - first)
+    if width < HALF:
+        d_ref[:, HALF - 128:] = jnp.zeros((2 * rows, 128), jnp.bfloat16)
+    for block, (x, u_ref) in enumerate(((x_ref, up_ref), (y_ref, upp_ref))):
+        at = slice(rows * block, rows * block + rows)
+        z = z_ref[at] + jnp.dot(x[:, 512:], w_ref[...], preferred_element_type=jnp.float32)
+        z = z[:, :width]
+        s = 1.0 / (1.0 + jnp.exp(-z))
+        d = u_ref[:, first:first + width].astype(jnp.float32) * s * (1.0 + z * (1.0 - s))
+        d_ref[at, :width] = d.astype(jnp.bfloat16)
+
+
+def forward(part, x, y, w, z, up, up_other):
+    rows = up.shape[0]
+    return pl.pallas_call(
+        functools.partial(forward_kernel, part),
+        in_specs=[vmem()] * 6,
+        out_specs=vmem(),
+        out_shape=jax.ShapeDtypeStruct((2 * rows, HALF), jnp.bfloat16),
+        compiler_params=params(20),
         cost_estimate=pl.CostEstimate(
-            flops=4 * terms * rows * 512 * LANES, bytes_accessed=4 << 20, transcendentals=0
+            flops=4 * rows * 512 * HALF, bytes_accessed=3 << 20, transcendentals=2 * rows * HALF
         ),
-    )(*ops)
-
-
-def forward_kernel(x_ref, xp_ref, w_ref, z_ref, up_ref, upp_ref, d_ref):
-    rows, cols = up_ref.shape
-    for block, (x, u_ref) in enumerate(((x_ref, up_ref), (xp_ref, upp_ref))):
-        at = slice(rows * block, rows * block + rows)
-        for n in range(2):
-            out = slice(HALF * n, HALF * n + HALF)
-            z = z_ref[at, out] + jnp.dot(x[:, 512:], w_ref[:, out], preferred_element_type=jnp.float32)
-            width = min(HALF, cols - HALF * n)
-            z = z[:, :width]
-            s = 1.0 / (1.0 + jnp.exp(-z))
-            up = u_ref[:, HALF * n:HALF * n + width].astype(jnp.float32)
-            d = up * s * (1.0 + z * (1.0 - s))
-            if width < HALF:
-                d_ref[at, LANES - 128:] = jnp.zeros((rows, 128), jnp.bfloat16)
-            d_ref[at, HALF * n:HALF * n + width] = d.astype(jnp.bfloat16)
-
-
-def forward(x, x_other, w, z, up, up_other):
-    rows, cols = up.shape
-    return pl.pallas_call(
-        forward_kernel,
-        in_specs=[vmem()] * 6,
-        out_specs=vmem(),
-        out_shape=jax.ShapeDtypeStruct((2 * rows, LANES), jnp.bfloat16),
-        compiler_params=params(24),
-        cost_estimate=pl.CostEstimate(
-            flops=4 * rows * 512 * cols, bytes_accessed=4 << 20, transcendentals=2 * rows * cols
-        ),
-        name="forward",
-    )(x, x_other, w, z, up, up_other)
-
-
-def back_kernel(width, sid_ref, d_ref, a0, a1, b0, b1, out_ref, wv):
+    )(x, y, w, z, up, up_other)
+
+
+def back_kernel(width, sid_ref, da_ref, db_ref, h0, fa0, fb0, h1, fa1, fb1, out_ref, wv):
     cx, _, core = place(sid_ref[0])
     rows = out_ref.shape[0]
-    for k, src in enumerate((a0, a1, b0, b1)):
-        c = core if k < 2 else 1 - core
-        for jx in range(2):
-            for jy in range(4):
-                bx = cx ^ mask_of(c, jx + 2 * (k % 2))
-                row = pl.multiple_of(((bx * NY + jy) * 2 + c) * ROWS, ROWS)
-                at = (jx * 4 + jy) * ROWS
-                wv[pl.ds(row, ROWS), :] = src[at:at + ROWS, :]
+    for c, held, fars in ((core, h0, (fa0, fb0)), (1 - core, h1, (fa1, fb1))):
+        for j in range(NX):
+            bx = cx ^ mask_of(c, j)
+            for by in range(NY):
+                to = pl.ds(pl.multiple_of(((bx * NY + by) * 2 + c) * ROWS, ROWS), ROWS)
+                at = ((j % 2) * NY + by) * ROWS
+                if j < 2:
+                    wv[to, :] = held[at:at + ROWS, :]
+                else:
+                    for i, far in enumerate(fars):
+                        wv[to, HALF * i:HALF * i + HALF] = far[at:at + ROWS, :]
     dims = (((1,), (1,)), ((), ()))
     for n in range(4):
-        g = lax.dot_general(
-            d_ref[:rows], wv[512 * n:512 * n + 512], dims, preferred_element_type=jnp.float32
-        )
+        at = slice(512 * n, 512 * n + 512)
+        g = lax.dot_general(da_ref[:rows], wv[at, :HALF], dims, preferred_element_type=jnp.float32)
+        g = g + lax.dot_general(db_ref[:rows], wv[at, HALF:], dims, preferred_element_type=jnp.float32)
         take = min(512, width - 512 * n)
         out_ref[:, 512 * n:512 * n + take] = g[:, :take].astype(jnp.bfloat16)
 
 
-def back(sid, rows, width, d, a0, a1, b0, b1):
+def back(sid, rows, width, d, pieces):
     return pl.pallas_call(
         functools.partial(back_kernel, width),
-        in_specs=[smem()] + [vmem()] * 5,
+        in_specs=[smem()] + [vmem()] * 8,
         out_specs=vmem(),
         out_shape=jax.ShapeDtypeStruct((rows, width), jnp.bfloat16),
         scratch_shapes=[pltpu.VMEM((2048, LANES), jnp.bfloat16)],
         compiler_params=params(20),
         cost_estimate=pl.CostEstimate(flops=2 * rows * 2048 * LANES, bytes_accessed=8 << 20, transcendentals=0),
         name="back",
-    )(sid, d, a0, a1, b0, b1)
-
-
-def partial_kernel(first, part, x_ref, xp_ref, d_ref, out_ref):
+    )(sid, *d, *pieces)
+
+
+def partial_kernel(first, x_ref, xp_ref, d_ref, out_ref):
     dims = (((0,), (0,)), ((), ()))
     rows = x_ref.shape[0]
     columns = slice(256 * first, 256 * first + 512)
-    out = slice(HALF * part, HALF * part + HALF)
-    r = lax.dot_general(x_ref[:, columns], d_ref[:rows, out], dims, preferred_element_type=jnp.float32)
-    r = r + lax.dot_general(xp_ref[:, columns], d_ref[rows:, out], dims, preferred_element_type=jnp.float32)
+    r = lax.dot_general(x_ref[:, columns], d_ref[:rows], dims, preferred_element_type=jnp.float32)
+    r = r + lax.dot_general(xp_ref[:, columns], d_ref[rows:], dims, preferred_element_type=jnp.float32)
     out_ref[...] = r.astype(jnp.bfloat16)
 
 
-def partial(first, part, x, x_other, d):
+def partial(first, x, x_other, d):
     rows = d.shape[0]
     return pl.pallas_call(
-        functools.partial(partial_kernel, first, part),
+        functools.partial(partial_kernel, first),
         in_specs=[vmem()] * 3,
         out_specs=vmem(),
         out_shape=jax.ShapeDtypeStruct((512, HALF), jnp.bfloat16),
@@ -348,22 +360,27 @@
     got, xa, xb = lax.optimization_barrier((got, xa, xb))
     held = jnp.concatenate([held, got])
     up_other = send(up_rows, "core")
-    far = send(held, "x", 2)
+    far = []
+    for i in range(2):
+        far.append(send(held[:, HALF * i:HALF * i + HALF], "x", 2))
     other_held = send(held, "core")
     ya, yb = split_by_core(sid, x_other)
-    z = product(0, (xa, ya, xb, yb), (held, other_held))
-    far, z, up_other = lax.optimization_barrier((far, z, up_other))
-    other_far = send(far, "core")
-    weights = (held, far, other_held, other_far)
-    z = product(512, (xa, ya), (far,), z)
-    d_pre = forward(xb, yb, other_far, z, up_rows, up_other)
-    got = [send(partial(2, i, xa, ya, d_pre), "x", 2) for i in range(2)]
-    keep = [partial(0, i, xa, ya, d_pre) for i in range(2)]
+    z = product(xa, ya, xb, yb, held, other_held)
+    far[0], z, up_other = lax.optimization_barrier((far[0], z, up_other))
+    other_far, d_pre, got = [], [], []
+    for i in range(2):
+        other_far.append(send(far[i], "core"))
+        zi = product_far(i, xa, ya, far[i], z)
+        d_pre.append(forward(i, xb, yb, other_far[i], zi, up_rows, up_other))
+        got.append(send(partial(2, xa, ya, d_pre[i]), "x", 2))
+    keep = [partial(0, xa, ya, d_pre[i]) for i in range(2)]
+    weights = (held, *far, other_held, *other_far)
     sums = []
     for i in range(2):
         (k0, k1), (g0, g1) = halves(keep[i]), halves(got[i])
-        sums.extend([add(k0, g0), send(add(k1, g1), "x", 1)])
-    grad_in = back(sid, x_rows.shape[0], in_width, d_pre, *weights)
+        sums.append(add(k0, g0))
+        sums.append(send(add(k1, g1), "x", 1))
+    grad_in = back(sid, x_rows.shape[0], in_width, d_pre, weights)
     sums[3], grad_in = lax.optimization_barrier((sums[3], grad_in))
 
     tokens = x_rows.shape[0] * n_shard

time: 137 us -> 138 us (level)
  the two profiles are of different devices: /device:TPU:6 before, /device:TPU:8 now
where the time goes in v1:
time: 138 us
  starting transfers between devices  47.1 us (34%)
  waiting for transfers between devices  34.9 us (25%)
  blocking collectives  32.6 us (24%)
  Pallas kernels  18 us (13%)
  between operations  2.39 us (2%)
  local copies, waits for them, and re-layouts  1.65 us (1%)
    ppermute x12, starting transfers between devices, send(): return lax.ppermute(v, 'shard', pairs(axis, stage))  32.7 us
    ppermute x12, waiting for transfers between devices, send(): return lax.ppermute(v, 'shard', pairs(axis, stage))  21.9 us
    all_gather x1, blocking collectives, body(): lax.all_gather(debiased, 'shard', axis=0, axis_index_groups=columns, tile...  18.3 us
    all_to_all x1, starting transfers between devices, body(): lax.all_to_all(pieces, ('gossip', 'shard'), split_axis=0, concat_axis=0,...  14.3 us
    all_to_all x1, blocking collectives, body(): lax.all_to_all(outgoing, 'gossip', split_axis=0, concat_axis=0, tiled=True)  14.3 us
    all_to_all x1, waiting for transfers between devices, body(): lax.all_to_all(pieces, ('gossip', 'shard'), split_axis=0, concat_axis=0,...  13 us
    pallas_call x2, Pallas kernels, split_by_core(): pl.pallas_call(split_kernel, in_specs=[smem(), vmem()], out_specs=[vmem()...  3.56 us
    pallas_call x1, Pallas kernels, back(): pl.pallas_call(functools.partial(back_kernel, width), in_specs=[smem()] +...  3.52 us
  transfers between devices with their start and end apart: 13, of which 6 were waited for; matrix products, arithmetic and copies ran while one was open for 0% of the time, Pallas kernels for 11%

profile of v1, /device:TPU:8, one launch (start us, length us, event | category | flops | bytes accessed | tf_op | source)
XLA Modules:
  0.0 137.9 jit_solution(446145779436898131)
XLA Ops:
  1.3 1.0 divide_convert_fusion
  2.3 18.3 %all_gather.3 = bf16[256,1024]{1,0:T(8,128)(2,1)S(1)} all-gather(bf16[64,1024]{1,0:T(8,128)(2,1)S(1)} %pad.4), channel_id=1, replica_groups={{0,2,4,6},{1,3,5,7},{8,10,12,14},{9,11,13,15},{16,18,20,22},{17,19,21,2..., dimensions={0}, use_global_device_ids=true | all-gather | bytes 655360 | tf_op jit(solution)/shard_map/all_gather | solution.py:355
  20.6 1.9 %collective-permute-start.1 = (bf16[432,2020]{1,0:T(8,128)(2,1)}, bf16[432,2020]{1,0:T(8,128)(2,1)S(1)}, u32[]{:S(2)}, u32[]{:S(2)}) collective-permute-start(bf16[432,2020]{1,0:T(8,128)(2,1)} %bitcast.13), channel_id=1, source_target_pairs={{0,1},{1,0},{2,3},{3,2},{4,5},{5,4},{6,7},{7,6},{8,9},{9,8},{10,11... | collective-permute-start | bytes 5235848 | tf_op jit(solution)/shard_map/ppermute | solution.py:41
  22.5 3.7 %collective-permute-start = (bf16[256,1024]{1,0:T(8,128)(2,1)S(1)}, bf16[256,1024]{1,0:T(8,128)(2,1)S(1)}, u32[]{:S(2)}, u32[]{:S(2)}) collective-permute-start(bf16[256,1024]{1,0:T(8,128)(2,1)S(1)} %all_gather.3), channel_id=1, source_target_pairs={{0,8},{1,25},{2,10},{3,27},{4,12},{5,29},{6,14},{7,31},{8,0},{9,17... | collective-permute-start | bytes 1572872 | tf_op jit(solution)/shard_map/ppermute | solution.py:41
  26.3 1.5 %copy-done.1 = bf16[1,432,2020]{2,1,0:T(8,128)(2,1)S(1)} copy-done((bf16[1,432,2020]{2,1,0:T(8,128)(2,1)S(1)}, bf16[1,432,2020]{2,1,0:T(8,128)(2,1)}, u32[]{:S(2)}) %copy-start.1) | copy-done | bytes 1745304
  27.7 1.8 %shard_map.85 = (bf16[432,1024]{1,0:T(8,128)(2,1)S(1)}, bf16[432,1024]{1,0:T(8,128)(2,1)S(1)}) custom-call(s32[1]{0:T(128)} %bitcast.4.sid_ref, bf16[432,2020]{1,0:T(8,128)(2,1)S(1)} %bitcast.14), custom_call_target="tpu_custom_call" | custom-call | flops 3538944 | bytes 3538944 | tf_op jit(solution)/shard_map/pallas_call | solution.py:79
  29.6 4.0 %collective-permute-done = bf16[256,1024]{1,0:T(8,128)(2,1)S(1)} collective-permute-done((bf16[256,1024]{1,0:T(8,128)(2,1)S(1)}, bf16[256,1024]{1,0:T(8,128)(2,1)S(1)}, u32[]{:S(2)}, u32[]{:S(2)}) %collective-permute-start) | collective-permute-done | bytes 524320 | tf_op jit(solution)/shard_map/ppermute | solution.py:41
  33.6 2.6 %collective-permute-start.5 = (bf16[512,1024]{1,0:T(8,128)(2,1)S(1)}, bf16[512,1024]{1,0:T(8,128)(2,1)S(1)}, u32[]{:S(2)}, u32[]{:S(2)}) collective-permute-start(bf16[512,1024]{1,0:T(8,128)(2,1)S(1)} %constant_dynamic-update-slice_fusion.wa_ref.h0), channel_id=1, source_target_pairs={{0,1},{1,0},{2,3},{3,2},{4,5},{5,4},{6,7},{7,6},{8,9},{9,8},{10,11... | collective-permute-start | bytes 3145736 | tf_op jit(solution)/shard_map/ppermute | solution.py:41
  36.3 1.9 %collective-permute-start.6 = (bf16[432,1010]{1,0:T(8,128)(2,1)S(1)}, bf16[432,1010]{1,0:T(8,128)(2,1)S(1)}, u32[]{:S(2)}, u32[]{:S(2)}) collective-permute-start(bf16[432,1010]{1,0:T(8,128)(2,1)S(1)} %bitcast.10), channel_id=1, source_target_pairs={{0,1},{1,0},{2,3},{3,2},{4,5},{5,4},{6,7},{7,6},{8,9},{9,8},{10,11... | collective-permute-start | bytes 2617928 | tf_op jit(solution)/shard_map/ppermute | solution.py:41
  38.3 4.9 %collective-permute-start.2 = (bf16[512,512]{1,0:T(8,128)(2,1)S(1)}, bf16[512,512]{1,0:T(8,128)(2,1)S(1)}, u32[]{:S(2)}, u32[]{:S(2)}) collective-permute-start(bf16[512,512]{1,0:T(8,128)(2,1)S(1)} %get-tuple-element.46), channel_id=1, source_target_pairs={{0,24},{1,9},{2,26},{3,11},{4,28},{5,13},{6,30},{7,15},{8,16},{9,1... | collective-permute-start | bytes 1572872 | tf_op jit(solution)/shard_map/ppermute | solution.py:41
  43.1 2.2 %collective-permute-start.4 = (bf16[512,512]{1,0:T(8,128)(2,1)S(1)}, bf16[512,512]{1,0:T(8,128)(2,1)S(1)}, u32[]{:S(2)}, u32[]{:S(2)}) collective-permute-start(bf16[512,512]{1,0:T(8,128)(2,1)S(1)} %get-tuple-element.45), channel_id=1, source_target_pairs={{0,24},{1,9},{2,26},{3,11},{4,28},{5,13},{6,30},{7,15},{8,16},{9,1... | collective-permute-start | bytes 1572872 | tf_op jit(solution)/shard_map/ppermute | solution.py:41
  45.3 5.2 %collective-permute-done.2.w_ref.fb0 = bf16[512,512]{1,0:T(8,128)(2,1)S(1)} collective-permute-done((bf16[512,512]{1,0:T(8,128)(2,1)S(1)}, bf16[512,512]{1,0:T(8,128)(2,1)S(1)}, u32[]{:S(2)}, u32[]{:S(2)}) %collective-permute-start.2) | collective-permute-done | bytes 524320 | tf_op jit(solution)/shard_map/ppermute | solution.py:41
  50.6 1.9 %collective-permute-start.3 = (bf16[512,512]{1,0:T(8,128)(2,1)S(1)}, bf16[512,512]{1,0:T(8,128)(2,1)S(1)}, u32[]{:S(2)}, u32[]{:S(2)}) collective-permute-start(bf16[512,512]{1,0:T(8,128)(2,1)S(1)} %collective-permute-done.2.w_ref.fb0), channel_id=1, source_target_pairs={{0,1},{1,0},{2,3},{3,2},{4,5},{5,4},{6,7},{7,6},{8,9},{9,8},{10,11... | collective-permute-start | bytes 1572872 | tf_op jit(solution)/shard_map/ppermute | solution.py:41
  52.5 1.8 %shard_map.86 = (bf16[432,1024]{1,0:T(8,128)(2,1)S(1)}, bf16[432,1024]{1,0:T(8,128)(2,1)S(1)}) custom-call(s32[1]{0:T(128)} %bitcast.4.sid_ref, bf16[432,2020]{1,0:T(8,128)(2,1)S(1)} %collective-permute-done.1.x_ref), custom_call_target="tpu_custom_call" | custom-call | flops 3538944 | bytes 3538944 | tf_op jit(solution)/shard_map/pallas_call | solution.py:79
  54.3 2.0 %product_held.1.z_ref = f32[864,1024]{1,0:T(8,128)S(1)} custom-call(bf16[432,1024]{1,0:T(8,128)(2,1)S(1)} %get-tuple-element.26.xa_ref.x_ref, bf16[432,1024]{1,0:T(8,128)(2,1)S(1)} %get-tuple-element.27.ya_ref.y_ref.xp_ref, bf16[432,1024]{1,0:T(8,128)(2,1)S(1)} %get-tuple-element.28.xb_ref.x_ref, bf16[432,1024]{1,0:T(8,128)(2,1)S(1)} %get-tuple-element.29.yb_ref.y_ref, ...), custom_call_target="tpu_custom_call" | custom-call | flops 1811939328 | bytes 4194304 | tf_op jit(solution)/shard_map/product_held/pallas_call | solution.py:102
  56.3 2.4 %collective-permute-start.9 = (bf16[512,512]{1,0:T(8,128)(2,1)S(1)}, bf16[512,512]{1,0:T(8,128)(2,1)S(1)}, u32[]{:S(2)}, u32[]{:S(2)}) collective-permute-start(bf16[512,512]{1,0:T(8,128)(2,1)S(1)} %collective-permute-done.4.w_ref.fa0), channel_id=1, source_target_pairs={{0,1},{1,0},{2,3},{3,2},{4,5},{5,4},{6,7},{7,6},{8,9},{9,8},{10,11... | collective-permute-start | bytes 1572872 | tf_op jit(solution)/shard_map/ppermute | solution.py:41
  59.4 1.1 shard_map.88.d_ref.db_ref
  61.3 4.9 %collective-permute-start.7 = (bf16[512,512]{1,0:T(8,128)(2,1)S(1)}, bf16[512,512]{1,0:T(8,128)(2,1)S(1)}, u32[]{:S(2)}, u32[]{:S(2)}) collective-permute-start(bf16[512,512]{1,0:T(8,128)(2,1)S(1)} %shard_map.90), channel_id=1, source_target_pairs={{0,24},{1,9},{2,26},{3,11},{4,28},{5,13},{6,30},{7,15},{8,16},{9,1... | collective-permute-start | bytes 1572872 | tf_op jit(solution)/shard_map/ppermute | solution.py:41
  66.8 1.1 shard_map.92.da_ref.d_ref
  68.7 2.2 %collective-permute-start.10 = (bf16[512,512]{1,0:T(8,128)(2,1)S(1)}, bf16[512,512]{1,0:T(8,128)(2,1)S(1)}, u32[]{:S(2)}, u32[]{:S(2)}) collective-permute-start(bf16[512,512]{1,0:T(8,128)(2,1)S(1)} %shard_map.94), channel_id=1, source_target_pairs={{0,24},{1,9},{2,26},{3,11},{4,28},{5,13},{6,30},{7,15},{8,16},{9,1... | collective-permute-start | bytes 1572872 | tf_op jit(solution)/shard_map/ppermute | solution.py:41
  70.9 0.7 shard_map.89
  71.6 1.9 %collective-permute-done.7 = bf16[512,512]{1,0:T(8,128)(2,1)S(1)} collective-permute-done((bf16[512,512]{1,0:T(8,128)(2,1)S(1)}, bf16[512,512]{1,0:T(8,128)(2,1)S(1)}, u32[]{:S(2)}, u32[]{:S(2)}) %collective-permute-start.7) | collective-permute-done | bytes 524320 | tf_op jit(solution)/shard_map/ppermute | solution.py:41
  73.7 1.9 %collective-permute-start.8 = (bf16[256,512]{1,0:T(8,128)(2,1)S(1)}, bf16[256,512]{1,0:T(8,128)(2,1)S(1)}, u32[]{:S(2)}, u32[]{:S(2)}) collective-permute-start(bf16[256,512]{1,0:T(8,128)(2,1)S(1)} %get-tuple-element.42), channel_id=1, source_target_pairs={{0,8},{1,25},{2,10},{3,27},{4,12},{5,29},{6,14},{7,31},{8,0},{9,17... | collective-permute-start | bytes 786440 | tf_op jit(solution)/shard_map/ppermute | solution.py:41
  76.3 8.1 %collective-permute-done.10 = bf16[512,512]{1,0:T(8,128)(2,1)S(1)} collective-permute-done((bf16[512,512]{1,0:T(8,128)(2,1)S(1)}, bf16[512,512]{1,0:T(8,128)(2,1)S(1)}, u32[]{:S(2)}, u32[]{:S(2)}) %collective-permute-start.10) | collective-permute-done | bytes 524320 | tf_op jit(solution)/shard_map/ppermute | solution.py:41
  84.6 2.2 %collective-permute-start.11 = (bf16[256,512]{1,0:T(8,128)(2,1)S(1)}, bf16[256,512]{1,0:T(8,128)(2,1)S(1)}, u32[]{:S(2)}, u32[]{:S(2)}) collective-permute-start(bf16[256,512]{1,0:T(8,128)(2,1)S(1)} %get-tuple-element.43), channel_id=1, source_target_pairs={{0,8},{1,25},{2,10},{3,27},{4,12},{5,29},{6,14},{7,31},{8,0},{9,17... | collective-permute-start | bytes 786440 | tf_op jit(solution)/shard_map/ppermute | solution.py:41
  86.8 3.5 %back.1 = bf16[432,2020]{1,0:T(8,128)(2,1)} custom-call(s32[1]{0:T(128)} %bitcast.4.sid_ref, bf16[864,512]{1,0:T(8,128)(2,1)S(1)} %shard_map.92.da_ref.d_ref, bf16[864,512]{1,0:T(8,128)(2,1)S(1)} %shard_map.88.d_ref.db_ref, bf16[512,1024]{1,0:T(8,128)(2,1)S(1)} %constant_dynamic-update-slice_fusion.wa_ref.h0, ...), custom_call_target="tpu_custom_call" | custom-call | flops 1811939328 | bytes 8388608 | tf_op jit(solution)/shard_map/back/pallas_call | solution.py:188
  90.3 2.6 %collective-permute-done.11.ga_ref = bf16[256,512]{1,0:T(8,128)(2,1)S(1)} collective-permute-done((bf16[256,512]{1,0:T(8,128)(2,1)S(1)}, bf16[256,512]{1,0:T(8,128)(2,1)S(1)}, u32[]{:S(2)}, u32[]{:S(2)}) %collective-permute-start.11) | collective-permute-done | bytes 262176 | tf_op jit(solution)/shard_map/ppermute | solution.py:41
  93.0 1.0 pack.1
  94.0 14.3 %all-to-all-start = ((bf16[64,32,128]{2,1,0:T(8,128)(2,1)}), bf16[64,32,128]{2,1,0:T(8,128)(2,1)S(1)}, u32[]{:S(2)}, u32[]{:S(2)}) async-start(bf16[64,32,128]{2,1,0:T(8,128)(2,1)} %get-tuple-element.38), calls=%async_computation | async-start | bytes 1048576 | tf_op jit(solution)/shard_map/all_to_all | solution.py:393
  109.0 13.0 %all-to-all-done.in_ref = bf16[64,32,128]{2,1,0:T(8,128)(2,1)S(1)} async-done(((bf16[64,32,128]{2,1,0:T(8,128)(2,1)}), bf16[64,32,128]{2,1,0:T(8,128)(2,1)S(1)}, u32[]{:S(2)}, u32[]{:S(2)}) %all-to-all-start) | async-done | bytes 524320 | tf_op jit(solution)/shard_map/all_to_all | solution.py:393
  122.7 14.3 %all_to_all.10.got_ref = bf16[16,32,128]{2,1,0:T(8,128)(2,1)S(1)} all-to-all(bf16[16,32,128]{2,1,0:T(8,128)(2,1)S(1)} %mix.1), channel_id=1, replica_groups=mesh['gossip'=16,'shard'=32] {'gossip'}, dimensions={0} | all-to-all | bytes 262144 | tf_op jit(solution)/shard_map/all_to_all | solution.py:397
  137.0 0.7 finish.1
  (26 shorter events, 4.6 us)
Async XLA Ops:
  20.6 31.9 %collective-permute-start.1 = (bf16[432,2020]{1,0:T(8,128)(2,1)}, bf16[432,2020]{1,0:T(8,128)(2,1)S(1)}, u32[]{:S(2)}, u32[]{:S(2)}) collective-permute-start(bf16[432,2020]{1,0:T(8,128)(2,1)} %bitcast.13), channel_id=1, source_target_pairs={{0,1},{1,0},{2,3},{3,2},{4,5},{5,4},{6,7},{7,6},{8,9},{9,8},{10,11... | collective-permute-start | bytes 5235848 | tf_op jit(solution)/shard_map/ppermute | solution.py:41
  22.5 11.1 %collective-permute-start = (bf16[256,1024]{1,0:T(8,128)(2,1)S(1)}, bf16[256,1024]{1,0:T(8,128)(2,1)S(1)}, u32[]{:S(2)}, u32[]{:S(2)}) collective-permute-start(bf16[256,1024]{1,0:T(8,128)(2,1)S(1)} %all_gather.3), channel_id=1, source_target_pairs={{0,8},{1,25},{2,10},{3,27},{4,12},{5,29},{6,14},{7,31},{8,0},{9,17... | collective-permute-start | bytes 1572872 | tf_op jit(solution)/shard_map/ppermute | solution.py:41
  26.3 1.5 %copy-start.1 = (bf16[1,432,2020]{2,1,0:T(8,128)(2,1)S(1)}, bf16[1,432,2020]{2,1,0:T(8,128)(2,1)}, u32[]{:S(2)}) copy-start(bf16[1,432,2020]{2,1,0:T(8,128)(2,1)} %param.6) | copy-start | bytes 5235844
  27.7 8.5 %copy-start = (bf16[1,432,1010]{2,1,0:T(8,128)(2,1)S(1)}, bf16[1,432,1010]{2,1,0:T(8,128)(2,1)}, u32[]{:S(2)}) copy-start(bf16[1,432,1010]{2,1,0:T(8,128)(2,1)} %param.7) | copy-start | bytes 2617924
  33.6 20.6 %collective-permute-start.5 = (bf16[512,1024]{1,0:T(8,128)(2,1)S(1)}, bf16[512,1024]{1,0:T(8,128)(2,1)S(1)}, u32[]{:S(2)}, u32[]{:S(2)}) collective-permute-start(bf16[512,1024]{1,0:T(8,128)(2,1)S(1)} %constant_dynamic-update-slice_fusion.wa_ref.h0), channel_id=1, source_target_pairs={{0,1},{1,0},{2,3},{3,2},{4,5},{5,4},{6,7},{7,6},{8,9},{9,8},{10,11... | collective-permute-start | bytes 3145736 | tf_op jit(solution)/shard_map/ppermute | solution.py:41
  36.3 20.0 %collective-permute-start.6 = (bf16[432,1010]{1,0:T(8,128)(2,1)S(1)}, bf16[432,1010]{1,0:T(8,128)(2,1)S(1)}, u32[]{:S(2)}, u32[]{:S(2)}) collective-permute-start(bf16[432,1010]{1,0:T(8,128)(2,1)S(1)} %bitcast.10), channel_id=1, source_target_pairs={{0,1},{1,0},{2,3},{3,2},{4,5},{5,4},{6,7},{7,6},{8,9},{9,8},{10,11... | collective-permute-start | bytes 2617928 | tf_op jit(solution)/shard_map/ppermute | solution.py:41
  38.3 12.3 %collective-permute-start.2 = (bf16[512,512]{1,0:T(8,128)(2,1)S(1)}, bf16[512,512]{1,0:T(8,128)(2,1)S(1)}, u32[]{:S(2)}, u32[]{:S(2)}) collective-permute-start(bf16[512,512]{1,0:T(8,128)(2,1)S(1)} %get-tuple-element.46), channel_id=1, source_target_pairs={{0,24},{1,9},{2,26},{3,11},{4,28},{5,13},{6,30},{7,15},{8,16},{9,1... | collective-permute-start | bytes 1572872 | tf_op jit(solution)/shard_map/ppermute | solution.py:41
  43.1 13.2 %collective-permute-start.4 = (bf16[512,512]{1,0:T(8,128)(2,1)S(1)}, bf16[512,512]{1,0:T(8,128)(2,1)S(1)}, u32[]{:S(2)}, u32[]{:S(2)}) collective-permute-start(bf16[512,512]{1,0:T(8,128)(2,1)S(1)} %get-tuple-element.45), channel_id=1, source_target_pairs={{0,24},{1,9},{2,26},{3,11},{4,28},{5,13},{6,30},{7,15},{8,16},{9,1... | collective-permute-start | bytes 1572872 | tf_op jit(solution)/shard_map/ppermute | solution.py:41
  50.6 8.8 %collective-permute-start.3 = (bf16[512,512]{1,0:T(8,128)(2,1)S(1)}, bf16[512,512]{1,0:T(8,128)(2,1)S(1)}, u32[]{:S(2)}, u32[]{:S(2)}) collective-permute-start(bf16[512,512]{1,0:T(8,128)(2,1)S(1)} %collective-permute-done.2.w_ref.fb0), channel_id=1, source_target_pairs={{0,1},{1,0},{2,3},{3,2},{4,5},{5,4},{6,7},{7,6},{8,9},{9,8},{10,11... | collective-permute-start | bytes 1572872 | tf_op jit(solution)/shard_map/ppermute | solution.py:41
  56.3 10.5 %collective-permute-start.9 = (bf16[512,512]{1,0:T(8,128)(2,1)S(1)}, bf16[512,512]{1,0:T(8,128)(2,1)S(1)}, u32[]{:S(2)}, u32[]{:S(2)}) collective-permute-start(bf16[512,512]{1,0:T(8,128)(2,1)S(1)} %collective-permute-done.4.w_ref.fa0), channel_id=1, source_target_pairs={{0,1},{1,0},{2,3},{3,2},{4,5},{5,4},{6,7},{7,6},{8,9},{9,8},{10,11... | collective-permute-start | bytes 1572872 | tf_op jit(solution)/shard_map/ppermute | solution.py:41
  61.3 12.3 %collective-permute-start.7 = (bf16[512,512]{1,0:T(8,128)(2,1)S(1)}, bf16[512,512]{1,0:T(8,128)(2,1)S(1)}, u32[]{:S(2)}, u32[]{:S(2)}) collective-permute-start(bf16[512,512]{1,0:T(8,128)(2,1)S(1)} %shard_map.90), channel_id=1, source_target_pairs={{0,24},{1,9},{2,26},{3,11},{4,28},{5,13},{6,30},{7,15},{8,16},{9,1... | collective-permute-start | bytes 1572872 | tf_op jit(solution)/shard_map/ppermute | solution.py:41
  68.7 15.8 %collective-permute-start.10 = (bf16[512,512]{1,0:T(8,128)(2,1)S(1)}, bf16[512,512]{1,0:T(8,128)(2,1)S(1)}, u32[]{:S(2)}, u32[]{:S(2)}) collective-permute-start(bf16[512,512]{1,0:T(8,128)(2,1)S(1)} %shard_map.94), channel_id=1, source_target_pairs={{0,24},{1,9},{2,26},{3,11},{4,28},{5,13},{6,30},{7,15},{8,16},{9,1... | collective-permute-start | bytes 1572872 | tf_op jit(solution)/shard_map/ppermute | solution.py:41
  73.7 16.6 %collective-permute-start.8 = (bf16[256,512]{1,0:T(8,128)(2,1)S(1)}, bf16[256,512]{1,0:T(8,128)(2,1)S(1)}, u32[]{:S(2)}, u32[]{:S(2)}) collective-permute-start(bf16[256,512]{1,0:T(8,128)(2,1)S(1)} %get-tuple-element.42), channel_id=1, source_target_pairs={{0,8},{1,25},{2,10},{3,27},{4,12},{5,29},{6,14},{7,31},{8,0},{9,17... | collective-permute-start | bytes 786440 | tf_op jit(solution)/shard_map/ppermute | solution.py:41
  84.5 8.4 %copy-start.2 = (f32[1,64,1010]{2,1,0:T(8,128)S(1)}, f32[1,64,1010]{2,1,0:T(8,128)}, u32[]{:S(2)}) copy-start(f32[1,64,1010]{2,1,0:T(8,128)} %param.8) | copy-start | bytes 775684
  84.6 8.4 %collective-permute-start.11 = (bf16[256,512]{1,0:T(8,128)(2,1)S(1)}, bf16[256,512]{1,0:T(8,128)(2,1)S(1)}, u32[]{:S(2)}, u32[]{:S(2)}) collective-permute-start(bf16[256,512]{1,0:T(8,128)(2,1)S(1)} %get-tuple-element.43), channel_id=1, source_target_pairs={{0,8},{1,25},{2,10},{3,27},{4,12},{5,29},{6,14},{7,31},{8,0},{9,17... | collective-permute-start | bytes 786440 | tf_op jit(solution)/shard_map/ppermute | solution.py:41
  90.3 31.7 %copy-start.3 = (s32[16]{0:T(128)S(1)}, s32[16]{0:T(128)}, u32[]{:S(2)}) copy-start(s32[16]{0:T(128)} %order_ref.1) | copy-start | bytes 196
  94.0 28.0 %all-to-all-start = ((bf16[64,32,128]{2,1,0:T(8,128)(2,1)}), bf16[64,32,128]{2,1,0:T(8,128)(2,1)S(1)}, u32[]{:S(2)}, u32[]{:S(2)}) async-start(bf16[64,32,128]{2,1,0:T(8,128)(2,1)} %get-tuple-element.38), calls=%async_computation | async-start | bytes 1048576 | tf_op jit(solution)/shard_map/all_to_all | solution.py:393

commit v2 on v1

--- a/solution.py
+++ b/solution.py
@@ -13,6 +13,7 @@
 ROWS = 64
 LANES = 1024
 HALF = 512
+PARTS = ((0, 768), (768, 256))
 
 
 def mask_of(core, j):
@@ -112,7 +113,8 @@
 
 def product_far_kernel(part, x_ref, y_ref, w_ref, z_ref, out_ref):
     rows = x_ref.shape[0]
-    columns = slice(HALF * part, HALF * part + HALF)
+    first, width = PARTS[part]
+    columns = slice(first, first + width)
     for block, x in enumerate((x_ref, y_ref)):
         at = slice(rows * block, rows * block + rows)
         out_ref[at] = z_ref[at, columns] + jnp.dot(
@@ -126,18 +128,18 @@
         functools.partial(product_far_kernel, part),
         in_specs=[vmem()] * 4,
         out_specs=vmem(),
-        out_shape=jax.ShapeDtypeStruct((2 * rows, HALF), jnp.float32),
+        out_shape=jax.ShapeDtypeStruct((2 * rows, PARTS[part][1]), jnp.float32),
         compiler_params=params(16),
-        cost_estimate=pl.CostEstimate(flops=4 * rows * 512 * HALF, bytes_accessed=2 << 20, transcendentals=0),
+        cost_estimate=pl.CostEstimate(flops=4 * rows * 512 * PARTS[part][1], bytes_accessed=2 << 20, transcendentals=0),
     )(x, y, w, z)
 
 
 def forward_kernel(part, x_ref, y_ref, w_ref, z_ref, up_ref, upp_ref, d_ref):
     rows, cols = up_ref.shape
-    first = HALF * part
-    width = min(HALF, cols - first)
-    if width < HALF:
-        d_ref[:, HALF - 128:] = jnp.zeros((2 * rows, 128), jnp.bfloat16)
+    first, wide = PARTS[part]
+    width = min(wide, cols - first)
+    if width < wide:
+        d_ref[:, wide - 128:] = jnp.zeros((2 * rows, 128), jnp.bfloat16)
     for block, (x, u_ref) in enumerate(((x_ref, up_ref), (y_ref, upp_ref))):
         at = slice(rows * block, rows * block + rows)
         z = z_ref[at] + jnp.dot(x[:, 512:], w_ref[...], preferred_element_type=jnp.float32)
@@ -153,10 +155,12 @@
         functools.partial(forward_kernel, part),
         in_specs=[vmem()] * 6,
         out_specs=vmem(),
-        out_shape=jax.ShapeDtypeStruct((2 * rows, HALF), jnp.bfloat16),
+        out_shape=jax.ShapeDtypeStruct((2 * rows, PARTS[part][1]), jnp.bfloat16),
         compiler_params=params(20),
         cost_estimate=pl.CostEstimate(
-            flops=4 * rows * 512 * HALF, bytes_accessed=3 << 20, transcendentals=2 * rows * HALF
+            flops=4 * rows * 512 * PARTS[part][1],
+            bytes_accessed=3 << 20,
+            transcendentals=2 * rows * PARTS[part][1],
         ),
     )(x, y, w, z, up, up_other)
 
@@ -173,13 +177,13 @@
                 if j < 2:
                     wv[to, :] = held[at:at + ROWS, :]
                 else:
-                    for i, far in enumerate(fars):
-                        wv[to, HALF * i:HALF * i + HALF] = far[at:at + ROWS, :]
+                    for (first, wide), far in zip(PARTS, fars):
+                        wv[to, first:first + wide] = far[at:at + ROWS, :]
     dims = (((1,), (1,)), ((), ()))
     for n in range(4):
         at = slice(512 * n, 512 * n + 512)
-        g = lax.dot_general(da_ref[:rows], wv[at, :HALF], dims, preferred_element_type=jnp.float32)
-        g = g + lax.dot_general(db_ref[:rows], wv[at, HALF:], dims, preferred_element_type=jnp.float32)
+        g = lax.dot_general(da_ref[:rows], wv[at, :PARTS[1][0]], dims, preferred_element_type=jnp.float32)
+        g = g + lax.dot_general(db_ref[:rows], wv[at, PARTS[1][0]:], dims, preferred_element_type=jnp.float32)
         take = min(512, width - 512 * n)
         out_ref[:, 512 * n:512 * n + take] = g[:, :take].astype(jnp.bfloat16)
 
@@ -212,9 +216,9 @@
         functools.partial(partial_kernel, first),
         in_specs=[vmem()] * 3,
         out_specs=vmem(),
-        out_shape=jax.ShapeDtypeStruct((512, HALF), jnp.bfloat16),
+        out_shape=jax.ShapeDtypeStruct((512, d.shape[1]), jnp.bfloat16),
         compiler_params=params(16),
-        cost_estimate=pl.CostEstimate(flops=2 * rows * 512 * HALF, bytes_accessed=2 << 20, transcendentals=0),
+        cost_estimate=pl.CostEstimate(flops=2 * rows * 512 * d.shape[1], bytes_accessed=2 << 20, transcendentals=0),
     )(x, x_other, d)
 
 
@@ -362,7 +366,8 @@
     up_other = send(up_rows, "core")
     far = []
     for i in range(2):
-        far.append(send(held[:, HALF * i:HALF * i + HALF], "x", 2))
+        first, wide = PARTS[i]
+        far.append(send(held[:, first:first + wide], "x", 2))
     other_held = send(held, "core")
     ya, yb = split_by_core(sid, x_other)
     z = product(xa, ya, xb, yb, held, other_held)
@@ -380,8 +385,6 @@
         (k0, k1), (g0, g1) = halves(keep[i]), halves(got[i])
         sums.append(add(k0, g0))
         sums.append(send(add(k1, g1), "x", 1))
-    grad_in = back(sid, x_rows.shape[0], in_width, d_pre, weights)
-    sums[3], grad_in = lax.optimization_barrier((sums[3], grad_in))
 
     tokens = x_rows.shape[0] * n_shard
     gid = lax.axis_index("gossip").astype(jnp.int32).reshape(1)
@@ -393,6 +396,8 @@
     received = lax.all_to_all(
         pieces, ("gossip", "shard"), split_axis=0, concat_axis=0, axis_index_groups=planes, tiled=True
     )
+    grad_in = back(sid, x_rows.shape[0], in_width, d_pre, weights)
+    received, grad_in = lax.optimization_barrier((received, grad_in))
     outgoing = mix(sid, gid, step, cycle_order, received)
     arrived = lax.all_to_all(outgoing, "gossip", split_axis=0, concat_axis=0, tiled=True)
     new_params, new_weight = finish(ps_weight, own, arrived)

time: 138 us -> 150 us (1.087)
  local copies, waits for them, and re-layouts: 1.65 us -> 9.57 us
  starting transfers between devices: 47.1 us -> 50.4 us
    unnamed x9 -> x35, local copies, waits for them, and re-layouts: 1.52 us -> 9.42 us
    all_to_all x1, waiting for transfers between devices: 13 us -> 6.71 us  [body(): lax.all_to_all(pieces, ('gossip', 'shard'), split_axis=0, concat_axis=0,...]
    ppermute x12, waiting for transfers between devices: 21.9 us -> 27.7 us  [send(): return lax.ppermute(v, 'shard', pairs(axis, stage))]
    ppermute x12, starting transfers between devices: 32.7 us -> 35.9 us  [send(): return lax.ppermute(v, 'shard', pairs(axis, stage))]
  transfers between devices with their start and end apart: 13 -> 13, of which waited for: 6 -> 8; matrix products, arithmetic and copies ran while one was open for 0% -> 0% of each run, Pallas kernels for 11% -> 10%
where the time goes in v2:
time: 150 us; the launch traced here: 149 us
  starting transfers between devices  50.4 us (34%)
  waiting for transfers between devices  34.4 us (23%)
  blocking collectives  32.6 us (22%)
  Pallas kernels  18.6 us (12%)
  local copies, waits for them, and re-layouts  9.57 us (6%)
  between operations  2.46 us (2%)
    ppermute x12, starting transfers between devices, send(): return lax.ppermute(v, 'shard', pairs(axis, stage))  35.9 us
    ppermute x12, waiting for transfers between devices, send(): return lax.ppermute(v, 'shard', pairs(axis, stage))  27.7 us
    all_gather x1, blocking collectives, body(): lax.all_gather(debiased, 'shard', axis=0, axis_index_groups=columns, tile...  18.3 us
    all_to_all x1, starting transfers between devices, body(): lax.all_to_all(pieces, ('gossip', 'shard'), split_axis=0, concat_axis=0,...  14.5 us
    all_to_all x1, blocking collectives, body(): lax.all_to_all(outgoing, 'gossip', split_axis=0, concat_axis=0, tiled=True)  14.3 us
    unnamed x35, local copies, waits for them, and re-layouts  9.42 us
    all_to_all x1, waiting for transfers between devices, body(): lax.all_to_all(pieces, ('gossip', 'shard'), split_axis=0, concat_axis=0,...  6.71 us
    pallas_call x2, Pallas kernels, split_by_core(): pl.pallas_call(split_kernel, in_specs=[smem(), vmem()], out_specs=[vmem()...  5.03 us
  transfers between devices with their start and end apart: 13, of which 8 were waited for; matrix products, arithmetic and copies ran while one was open for 0% of the time, Pallas kernels for 10%

profile of v2, /device:TPU:8, one launch (start us, length us, event | category | flops | bytes accessed | tf_op | source)
XLA Modules:
  0.0 149.3 jit_solution(13630849336887521055)
XLA Ops:
  2.3 18.3 %all_gather.3 = bf16[256,1024]{1,0:T(8,128)(2,1)S(1)} all-gather(bf16[64,1024]{1,0:T(8,128)(2,1)S(1)} %pad.4), channel_id=1, replica_groups={{0,2,4,6},{1,3,5,7},{8,10,12,14},{9,11,13,15},{16,18,20,22},{17,19,21,2..., dimensions={0}, use_global_device_ids=true | all-gather | bytes 655360 | tf_op jit(solution)/shard_map/all_gather | solution.py:359
  20.6 1.9 %collective-permute-start.1 = (bf16[432,2020]{1,0:T(8,128)(2,1)}, bf16[432,2020]{1,0:T(8,128)(2,1)}, u32[]{:S(2)}, u32[]{:S(2)}) collective-permute-start(bf16[432,2020]{1,0:T(8,128)(2,1)} %bitcast.13), channel_id=1, source_target_pairs={{0,1},{1,0},{2,3},{3,2},{4,5},{5,4},{6,7},{7,6},{8,9},{9,8},{10,11... | collective-permute-start | bytes 5235848 | tf_op jit(solution)/shard_map/ppermute | solution.py:42
  22.5 3.7 %collective-permute-start = (bf16[256,1024]{1,0:T(8,128)(2,1)S(1)}, bf16[256,1024]{1,0:T(8,128)(2,1)S(1)}, u32[]{:S(2)}, u32[]{:S(2)}) collective-permute-start(bf16[256,1024]{1,0:T(8,128)(2,1)S(1)} %all_gather.3), channel_id=1, source_target_pairs={{0,8},{1,25},{2,10},{3,27},{4,12},{5,29},{6,14},{7,31},{8,0},{9,17... | collective-permute-start | bytes 1572872 | tf_op jit(solution)/shard_map/ppermute | solution.py:42
  26.3 1.5 copy-done.7
  27.7 1.8 %shard_map.85 = (bf16[432,1024]{1,0:T(8,128)(2,1)S(1)}, bf16[432,1024]{1,0:T(8,128)(2,1)S(1)}) custom-call(s32[1]{0:T(128)} %bitcast.sid_ref, bf16[432,2020]{1,0:T(8,128)(2,1)S(1)} %bitcast.14), custom_call_target="tpu_custom_call" | custom-call | flops 3538944 | bytes 3538944 | tf_op jit(solution)/shard_map/pallas_call | solution.py:80
  29.6 4.0 %collective-permute-done = bf16[256,1024]{1,0:T(8,128)(2,1)S(1)} collective-permute-done((bf16[256,1024]{1,0:T(8,128)(2,1)S(1)}, bf16[256,1024]{1,0:T(8,128)(2,1)S(1)}, u32[]{:S(2)}, u32[]{:S(2)}) %collective-permute-start) | collective-permute-done | bytes 524320 | tf_op jit(solution)/shard_map/ppermute | solution.py:42
  33.6 2.6 %collective-permute-start.3 = (bf16[512,1024]{1,0:T(8,128)(2,1)S(1)}, bf16[512,1024]{1,0:T(8,128)(2,1)S(1)}, u32[]{:S(2)}, u32[]{:S(2)}) collective-permute-start(bf16[512,1024]{1,0:T(8,128)(2,1)S(1)} %constant_dynamic-update-slice_fusion.wa_ref.h0), channel_id=1, source_target_pairs={{0,1},{1,0},{2,3},{3,2},{4,5},{5,4},{6,7},{7,6},{8,9},{9,8},{10,11... | collective-permute-start | bytes 3145736 | tf_op jit(solution)/shard_map/ppermute | solution.py:42
  36.3 1.9 %collective-permute-start.4 = (bf16[432,1010]{1,0:T(8,128)(2,1)S(1)}, bf16[432,1010]{1,0:T(8,128)(2,1)S(1)}, u32[]{:S(2)}, u32[]{:S(2)}) collective-permute-start(bf16[432,1010]{1,0:T(8,128)(2,1)S(1)} %bitcast.10), channel_id=1, source_target_pairs={{0,1},{1,0},{2,3},{3,2},{4,5},{5,4},{6,7},{7,6},{8,9},{9,8},{10,11... | collective-permute-start | bytes 2617928 | tf_op jit(solution)/shard_map/ppermute | solution.py:42
  38.3 4.9 %collective-permute-start.2 = (bf16[512,768]{1,0:T(8,128)(2,1)S(1)}, bf16[512,768]{1,0:T(8,128)(2,1)S(1)}, u32[]{:S(2)}, u32[]{:S(2)}) collective-permute-start(bf16[512,768]{1,0:T(8,128)(2,1)S(1)} %slice.40), channel_id=1, source_target_pairs={{0,24},{1,9},{2,26},{3,11},{4,28},{5,13},{6,30},{7,15},{8,16},{9,1... | collective-permute-start | bytes 2359304 | tf_op jit(solution)/shard_map/ppermute | solution.py:42
  43.1 3.3 %shard_map.86 = (bf16[432,1024]{1,0:T(8,128)(2,1)S(1)}, bf16[432,1024]{1,0:T(8,128)(2,1)S(1)}) custom-call(s32[1]{0:T(128)} %bitcast.sid_ref, bf16[432,2020]{1,0:T(8,128)(2,1)} %collective-permute-done.1.x_ref), custom_call_target="tpu_custom_call" | custom-call | flops 3538944 | bytes 3538944 | tf_op jit(solution)/shard_map/pallas_call | solution.py:80
  46.4 2.0 %product_held.1.z_ref = f32[864,1024]{1,0:T(8,128)S(1)} custom-call(bf16[432,1024]{1,0:T(8,128)(2,1)S(1)} %get-tuple-element.26.xa_ref.x_ref, bf16[432,1024]{1,0:T(8,128)(2,1)S(1)} %get-tuple-element.27.ya_ref.y_ref.xp_ref, bf16[432,1024]{1,0:T(8,128)(2,1)S(1)} %get-tuple-element.28.xb_ref.x_ref, bf16[432,1024]{1,0:T(8,128)(2,1)S(1)} %get-tuple-element.29.yb_ref.y_ref, ...), custom_call_target="tpu_custom_call" | custom-call | flops 1811939328 | bytes 4194304 | tf_op jit(solution)/shard_map/product_held/pallas_call | solution.py:103
  48.4 4.9 %collective-permute-done.2.w_ref.fa0 = bf16[512,768]{1,0:T(8,128)(2,1)S(1)} collective-permute-done((bf16[512,768]{1,0:T(8,128)(2,1)S(1)}, bf16[512,768]{1,0:T(8,128)(2,1)S(1)}, u32[]{:S(2)}, u32[]{:S(2)}) %collective-permute-start.2) | collective-permute-done | bytes 786464 | tf_op jit(solution)/shard_map/ppermute | solution.py:42
  53.4 1.9 %collective-permute-start.5 = (bf16[512,768]{1,0:T(8,128)(2,1)S(1)}, bf16[512,768]{1,0:T(8,128)(2,1)S(1)}, u32[]{:S(2)}, u32[]{:S(2)}) collective-permute-start(bf16[512,768]{1,0:T(8,128)(2,1)S(1)} %collective-permute-done.2.w_ref.fa0), channel_id=1, source_target_pairs={{0,1},{1,0},{2,3},{3,2},{4,5},{5,4},{6,7},{7,6},{8,9},{9,8},{10,11... | collective-permute-start | bytes 2359304 | tf_op jit(solution)/shard_map/ppermute | solution.py:42
  56.2 1.4 collective-permute-done.5.w_ref.fa1
  57.5 1.5 %shard_map.88.d_ref.da_ref = bf16[864,768]{1,0:T(8,128)(2,1)S(1)} custom-call(bf16[432,1024]{1,0:T(8,128)(2,1)S(1)} %get-tuple-element.28.xb_ref.x_ref, bf16[432,1024]{1,0:T(8,128)(2,1)S(1)} %get-tuple-element.29.yb_ref.y_ref, bf16[512,768]{1,0:T(8,128)(2,1)S(1)} %collective-permute-done.5.w_ref.fa1, f32[864,768]{1,0:T(8,128)S(1)} %shard_map.87.z_ref, ...), custom_call_target="tpu_custom_call" | custom-call | flops 679477248 | bytes 3145728 | tf_op jit(solution)/shard_map/pallas_call | solution.py:154
  59.1 1.0 shard_map.90
  60.1 4.9 %collective-permute-start.6 = (bf16[512,768]{1,0:T(8,128)(2,1)S(1)}, bf16[512,768]{1,0:T(8,128)(2,1)S(1)}, u32[]{:S(2)}, u32[]{:S(2)}) collective-permute-start(bf16[512,768]{1,0:T(8,128)(2,1)S(1)} %shard_map.90), channel_id=1, source_target_pairs={{0,24},{1,9},{2,26},{3,11},{4,28},{5,13},{6,30},{7,15},{8,16},{9,1... | collective-permute-start | bytes 2359304 | tf_op jit(solution)/shard_map/ppermute | solution.py:42
  65.0 2.2 %collective-permute-start.8 = (bf16[512,256]{1,0:T(8,128)(2,1)S(1)}, bf16[512,256]{1,0:T(8,128)(2,1)S(1)}, u32[]{:S(2)}, u32[]{:S(2)}) collective-permute-start(bf16[512,256]{1,0:T(8,128)(2,1)S(1)} %slice.45), channel_id=1, source_target_pairs={{0,24},{1,9},{2,26},{3,11},{4,28},{5,13},{6,30},{7,15},{8,16},{9,1... | collective-permute-start | bytes 786440 | tf_op jit(solution)/shard_map/ppermute | solution.py:42
  67.2 10.8 %collective-permute-done.8.w_ref.fb0 = bf16[512,256]{1,0:T(8,128)(2,1)S(1)} collective-permute-done((bf16[512,256]{1,0:T(8,128)(2,1)S(1)}, bf16[512,256]{1,0:T(8,128)(2,1)S(1)}, u32[]{:S(2)}, u32[]{:S(2)}) %collective-permute-start.8) | collective-permute-done | bytes 262176 | tf_op jit(solution)/shard_map/ppermute | solution.py:42
  78.0 1.9 %collective-permute-start.9 = (bf16[512,256]{1,0:T(8,128)(2,1)S(1)}, bf16[512,256]{1,0:T(8,128)(2,1)S(1)}, u32[]{:S(2)}, u32[]{:S(2)}) collective-permute-start(bf16[512,256]{1,0:T(8,128)(2,1)S(1)} %collective-permute-done.8.w_ref.fb0), channel_id=1, source_target_pairs={{0,1},{1,0},{2,3},{3,2},{4,5},{5,4},{6,7},{7,6},{8,9},{9,8},{10,11... | collective-permute-start | bytes 786440 | tf_op jit(solution)/shard_map/ppermute | solution.py:42
  80.3 1.1 collective-permute-done.9.w_ref.fb1
  82.7 4.9 %collective-permute-start.10 = (bf16[512,256]{1,0:T(8,128)(2,1)S(1)}, bf16[512,256]{1,0:T(8,128)(2,1)S(1)}, u32[]{:S(2)}, u32[]{:S(2)}) collective-permute-start(bf16[512,256]{1,0:T(8,128)(2,1)S(1)} %shard_map.94), channel_id=1, source_target_pairs={{0,24},{1,9},{2,26},{3,11},{4,28},{5,13},{6,30},{7,15},{8,16},{9,1... | collective-permute-start | bytes 786440 | tf_op jit(solution)/shard_map/ppermute | solution.py:42
  88.8 2.2 %collective-permute-start.7 = (bf16[256,768]{1,0:T(8,128)(2,1)S(1)}, bf16[256,768]{1,0:T(8,128)(2,1)S(1)}, u32[]{:S(2)}, u32[]{:S(2)}) collective-permute-start(bf16[256,768]{1,0:T(8,128)(2,1)S(1)} %get-tuple-element.41), channel_id=1, source_target_pairs={{0,8},{1,25},{2,10},{3,27},{4,12},{5,29},{6,14},{7,31},{8,0},{9,17... | collective-permute-start | bytes 1179656 | tf_op jit(solution)/shard_map/ppermute | solution.py:42
  92.4 3.0 %collective-permute-start.11 = (bf16[256,256]{1,0:T(8,128)(2,1)S(1)}, bf16[256,256]{1,0:T(8,128)(2,1)S(1)}, u32[]{:S(2)}, u32[]{:S(2)}) collective-permute-start(bf16[256,256]{1,0:T(8,128)(2,1)S(1)} %get-tuple-element.43), channel_id=1, source_target_pairs={{0,8},{1,25},{2,10},{3,27},{4,12},{5,29},{6,14},{7,31},{8,0},{9,17... | collective-permute-start | bytes 393224 | tf_op jit(solution)/shard_map/ppermute | solution.py:42
  95.3 4.6 %collective-permute-done.11.gb_ref = bf16[256,256]{1,0:T(8,128)(2,1)S(1)} collective-permute-done((bf16[256,256]{1,0:T(8,128)(2,1)S(1)}, bf16[256,256]{1,0:T(8,128)(2,1)S(1)}, u32[]{:S(2)}, u32[]{:S(2)}) %collective-permute-start.11) | collective-permute-done | bytes 131104 | tf_op jit(solution)/shard_map/ppermute | solution.py:42
  101.7 14.5 %all-to-all-start = ((bf16[64,32,128]{2,1,0:T(8,128)(2,1)}), bf16[64,32,128]{2,1,0:T(8,128)(2,1)S(1)}, u32[]{:S(2)}, u32[]{:S(2)}) async-start(bf16[64,32,128]{2,1,0:T(8,128)(2,1)} %copy-done.13), calls=%async_computation | async-start | bytes 1048576 | tf_op jit(solution)/shard_map/all_to_all | solution.py:396
  116.8 1.2 copy-done.1
  118.1 1.1 copy-done.4
  119.2 1.1 copy-done.6
  122.2 3.5 %back.1 = bf16[432,2020]{1,0:T(8,128)(2,1)} custom-call(s32[1]{0:T(128)} %bitcast.sid_ref, bf16[864,768]{1,0:T(8,128)(2,1)S(1)} %shard_map.88.d_ref.da_ref, bf16[864,256]{1,0:T(8,128)(2,1)S(1)} %shard_map.92.d_ref.db_ref, bf16[512,1024]{1,0:T(8,128)(2,1)S(1)} %constant_dynamic-update-slice_fusion.wa_ref.h0, bf16[512,768]{1,0:T(8,128)(2,1)S(1)} %copy-done.4, ...), custom_call_target="tpu_custom_call" | custom-call | flops 1811939328 | bytes 8388608 | tf_op jit(solution)/shard_map/back/pallas_call | solution.py:192
  125.7 6.7 %all-to-all-done.in_ref = bf16[64,32,128]{2,1,0:T(8,128)(2,1)S(1)} async-done(((bf16[64,32,128]{2,1,0:T(8,128)(2,1)}), bf16[64,32,128]{2,1,0:T(8,128)(2,1)S(1)}, u32[]{:S(2)}, u32[]{:S(2)}) %all-to-all-start) | async-done | bytes 524320 | tf_op jit(solution)/shard_map/all_to_all | solution.py:396
  133.1 14.3 %all_to_all.10.got_ref = bf16[16,32,128]{2,1,0:T(8,128)(2,1)S(1)} all-to-all(bf16[16,32,128]{2,1,0:T(8,128)(2,1)S(1)} %mix.1), channel_id=1, replica_groups=mesh['gossip'=16,'shard'=32] {'gossip'}, dimensions={0} | all-to-all | bytes 262144 | tf_op jit(solution)/shard_map/all_to_all | solution.py:402
  (53 shorter events, 12.2 us)
Async XLA Ops:
  20.6 22.5 %collective-permute-start.1 = (bf16[432,2020]{1,0:T(8,128)(2,1)}, bf16[432,2020]{1,0:T(8,128)(2,1)}, u32[]{:S(2)}, u32[]{:S(2)}) collective-permute-start(bf16[432,2020]{1,0:T(8,128)(2,1)} %bitcast.13), channel_id=1, source_target_pairs={{0,1},{1,0},{2,3},{3,2},{4,5},{5,4},{6,7},{7,6},{8,9},{9,8},{10,11... | collective-permute-start | bytes 5235848 | tf_op jit(solution)/shard_map/ppermute | solution.py:42
  22.5 11.1 %collective-permute-start = (bf16[256,1024]{1,0:T(8,128)(2,1)S(1)}, bf16[256,1024]{1,0:T(8,128)(2,1)S(1)}, u32[]{:S(2)}, u32[]{:S(2)}) collective-permute-start(bf16[256,1024]{1,0:T(8,128)(2,1)S(1)} %all_gather.3), channel_id=1, source_target_pairs={{0,8},{1,25},{2,10},{3,27},{4,12},{5,29},{6,14},{7,31},{8,0},{9,17... | collective-permute-start | bytes 1572872 | tf_op jit(solution)/shard_map/ppermute | solution.py:42
  26.3 1.5 copy-start.7
  27.7 8.5 %copy-start.2 = (bf16[1,432,1010]{2,1,0:T(8,128)(2,1)S(1)}, bf16[1,432,1010]{2,1,0:T(8,128)(2,1)}, u32[]{:S(2)}) copy-start(bf16[1,432,1010]{2,1,0:T(8,128)(2,1)} %param.7) | copy-start | bytes 2617924
  33.6 12.8 %collective-permute-start.3 = (bf16[512,1024]{1,0:T(8,128)(2,1)S(1)}, bf16[512,1024]{1,0:T(8,128)(2,1)S(1)}, u32[]{:S(2)}, u32[]{:S(2)}) collective-permute-start(bf16[512,1024]{1,0:T(8,128)(2,1)S(1)} %constant_dynamic-update-slice_fusion.wa_ref.h0), channel_id=1, source_target_pairs={{0,1},{1,0},{2,3},{3,2},{4,5},{5,4},{6,7},{7,6},{8,9},{9,8},{10,11... | collective-permute-start | bytes 3145736 | tf_op jit(solution)/shard_map/ppermute | solution.py:42
  36.3 12.2 %collective-permute-start.4 = (bf16[432,1010]{1,0:T(8,128)(2,1)S(1)}, bf16[432,1010]{1,0:T(8,128)(2,1)S(1)}, u32[]{:S(2)}, u32[]{:S(2)}) collective-permute-start(bf16[432,1010]{1,0:T(8,128)(2,1)S(1)} %bitcast.10), channel_id=1, source_target_pairs={{0,1},{1,0},{2,3},{3,2},{4,5},{5,4},{6,7},{7,6},{8,9},{9,8},{10,11... | collective-permute-start | bytes 2617928 | tf_op jit(solution)/shard_map/ppermute | solution.py:42
  38.3 15.1 %collective-permute-start.2 = (bf16[512,768]{1,0:T(8,128)(2,1)S(1)}, bf16[512,768]{1,0:T(8,128)(2,1)S(1)}, u32[]{:S(2)}, u32[]{:S(2)}) collective-permute-start(bf16[512,768]{1,0:T(8,128)(2,1)S(1)} %slice.40), channel_id=1, source_target_pairs={{0,24},{1,9},{2,26},{3,11},{4,28},{5,13},{6,30},{7,15},{8,16},{9,1... | collective-permute-start | bytes 2359304 | tf_op jit(solution)/shard_map/ppermute | solution.py:42
  46.4 2.0 %copy-start = (bf16[512,1024]{1,0:T(8,128)(2,1)}, bf16[512,1024]{1,0:T(8,128)(2,1)S(1)}, u32[]{:S(2)}) copy-start(bf16[512,1024]{1,0:T(8,128)(2,1)S(1)} %collective-permute-done.3.wb_ref.h1) | copy-start | bytes 3145732
  53.4 2.8 %copy-start.3 = (bf16[512,768]{1,0:T(8,128)(2,1)}, bf16[512,768]{1,0:T(8,128)(2,1)S(1)}, u32[]{:S(2)}) copy-start(bf16[512,768]{1,0:T(8,128)(2,1)S(1)} %collective-permute-done.2.w_ref.fa0) | copy-start | bytes 2359300
  53.4 4.2 %collective-permute-start.5 = (bf16[512,768]{1,0:T(8,128)(2,1)S(1)}, bf16[512,768]{1,0:T(8,128)(2,1)S(1)}, u32[]{:S(2)}, u32[]{:S(2)}) collective-permute-start(bf16[512,768]{1,0:T(8,128)(2,1)S(1)} %collective-permute-done.2.w_ref.fa0), channel_id=1, source_target_pairs={{0,1},{1,0},{2,3},{3,2},{4,5},{5,4},{6,7},{7,6},{8,9},{9,8},{10,11... | collective-permute-start | bytes 2359304 | tf_op jit(solution)/shard_map/ppermute | solution.py:42
  57.5 1.5 %copy-start.5 = (bf16[512,768]{1,0:T(8,128)(2,1)}, bf16[512,768]{1,0:T(8,128)(2,1)S(1)}, u32[]{:S(2)}) copy-start(bf16[512,768]{1,0:T(8,128)(2,1)S(1)} %collective-permute-done.5.w_ref.fa1) | copy-start | bytes 2359300
  60.1 28.4 %collective-permute-start.6 = (bf16[512,768]{1,0:T(8,128)(2,1)S(1)}, bf16[512,768]{1,0:T(8,128)(2,1)S(1)}, u32[]{:S(2)}, u32[]{:S(2)}) collective-permute-start(bf16[512,768]{1,0:T(8,128)(2,1)S(1)} %shard_map.90), channel_id=1, source_target_pairs={{0,24},{1,9},{2,26},{3,11},{4,28},{5,13},{6,30},{7,15},{8,16},{9,1... | collective-permute-start | bytes 2359304 | tf_op jit(solution)/shard_map/ppermute | solution.py:42
  65.0 13.0 %collective-permute-start.8 = (bf16[512,256]{1,0:T(8,128)(2,1)S(1)}, bf16[512,256]{1,0:T(8,128)(2,1)S(1)}, u32[]{:S(2)}, u32[]{:S(2)}) collective-permute-start(bf16[512,256]{1,0:T(8,128)(2,1)S(1)} %slice.45), channel_id=1, source_target_pairs={{0,24},{1,9},{2,26},{3,11},{4,28},{5,13},{6,30},{7,15},{8,16},{9,1... | collective-permute-start | bytes 786440 | tf_op jit(solution)/shard_map/ppermute | solution.py:42
  78.0 2.3 %copy-start.8 = (bf16[512,256]{1,0:T(8,128)(2,1)}, bf16[512,256]{1,0:T(8,128)(2,1)S(1)}, u32[]{:S(2)}) copy-start(bf16[512,256]{1,0:T(8,128)(2,1)S(1)} %collective-permute-done.8.w_ref.fb0) | copy-start | bytes 786436
  78.0 3.4 %collective-permute-start.9 = (bf16[512,256]{1,0:T(8,128)(2,1)S(1)}, bf16[512,256]{1,0:T(8,128)(2,1)S(1)}, u32[]{:S(2)}, u32[]{:S(2)}) collective-permute-start(bf16[512,256]{1,0:T(8,128)(2,1)S(1)} %collective-permute-done.8.w_ref.fb0), channel_id=1, source_target_pairs={{0,1},{1,0},{2,3},{3,2},{4,5},{5,4},{6,7},{7,6},{8,9},{9,8},{10,11... | collective-permute-start | bytes 786440 | tf_op jit(solution)/shard_map/ppermute | solution.py:42
  81.4 0.7 copy-start.10
  82.7 9.6 %collective-permute-start.10 = (bf16[512,256]{1,0:T(8,128)(2,1)S(1)}, bf16[512,256]{1,0:T(8,128)(2,1)S(1)}, u32[]{:S(2)}, u32[]{:S(2)}) collective-permute-start(bf16[512,256]{1,0:T(8,128)(2,1)S(1)} %shard_map.94), channel_id=1, source_target_pairs={{0,24},{1,9},{2,26},{3,11},{4,28},{5,13},{6,30},{7,15},{8,16},{9,1... | collective-permute-start | bytes 786440 | tf_op jit(solution)/shard_map/ppermute | solution.py:42
  88.7 11.2 %copy-start.12 = (f32[1,64,1010]{2,1,0:T(8,128)S(1)}, f32[1,64,1010]{2,1,0:T(8,128)}, u32[]{:S(2)}) copy-start(f32[1,64,1010]{2,1,0:T(8,128)} %param.8) | copy-start | bytes 775684
  88.8 11.2 %collective-permute-start.7 = (bf16[256,768]{1,0:T(8,128)(2,1)S(1)}, bf16[256,768]{1,0:T(8,128)(2,1)S(1)}, u32[]{:S(2)}, u32[]{:S(2)}) collective-permute-start(bf16[256,768]{1,0:T(8,128)(2,1)S(1)} %get-tuple-element.41), channel_id=1, source_target_pairs={{0,8},{1,25},{2,10},{3,27},{4,12},{5,29},{6,14},{7,31},{8,0},{9,17... | collective-permute-start | bytes 1179656 | tf_op jit(solution)/shard_map/ppermute | solution.py:42
  92.4 7.6 %collective-permute-start.11 = (bf16[256,256]{1,0:T(8,128)(2,1)S(1)}, bf16[256,256]{1,0:T(8,128)(2,1)S(1)}, u32[]{:S(2)}, u32[]{:S(2)}) collective-permute-start(bf16[256,256]{1,0:T(8,128)(2,1)S(1)} %get-tuple-element.43), channel_id=1, source_target_pairs={{0,8},{1,25},{2,10},{3,27},{4,12},{5,29},{6,14},{7,31},{8,0},{9,17... | collective-permute-start | bytes 393224 | tf_op jit(solution)/shard_map/ppermute | solution.py:42
  100.2 0.8 copy-start.13
  101.0 0.7 copy-start.14
  101.7 30.8 %all-to-all-start = ((bf16[64,32,128]{2,1,0:T(8,128)(2,1)}), bf16[64,32,128]{2,1,0:T(8,128)(2,1)S(1)}, u32[]{:S(2)}, u32[]{:S(2)}) async-start(bf16[64,32,128]{2,1,0:T(8,128)(2,1)} %copy-done.13), calls=%async_computation | async-start | bytes 1048576 | tf_op jit(solution)/shard_map/all_to_all | solution.py:396
  116.8 1.2 copy-start.1
  118.1 1.1 copy-start.4
  119.2 1.1 copy-start.6
  120.3 0.9 copy-start.9
  121.3 0.9 copy-start.11
  122.2 10.2 %copy-start.16 = (s32[16]{0:T(128)S(1)}, s32[16]{0:T(128)}, u32[]{:S(2)}) copy-start(s32[16]{0:T(128)} %order_ref.1) | copy-start | bytes 196
  147.4 1.0 copy-start.15
